TPU v7x, 32 devices: a whole 2x2x4 slice. The times are simulated.
32 devices in a mesh: order: 8 (over z, x), chan: 4 (over y, core).
Axes of the slice: x: 2, y: 2, z: 4, core: 2. Of those that a mesh axis runs over, the one named last changes fastest.
Arguments:
- cotangent: bfloat16 [248, 240, 1, 2, 1024], P('order', None, None, None, 'chan'), may hold values from -0.59765625 to 0.59765625
- stored_coefficients: bfloat16 [248, 240, 1, 2, 1024], P('order', None, None, None, 'chan'), may hold values from -0.29882812 to 0.29882812
- weights: bfloat16 [248, 1024, 1024], P('order', 'chan'), may hold values from -0.1875 to 0.1875
- order_table: int32 [248], replicated, may hold values from 0 to 240, as said below
- degree_table: int32 [248], replicated, may hold values from 0 to 240, as said below
Outputs:
- input_gradient: bfloat16 [248, 240, 1, 2, 1024], P('order', None, None, None, 'chan')
- mixing_gradient: bfloat16 [248, 1024, 1024], P('order', 'chan')
Inputs may be any that keep to these rules, and one draw needn't show every extreme that they name: `order_table`: each order 0 to 239 stands in exactly one slot; every other slot holds 240, meaning empty. `degree_table`: each degree 0 to 239 stands in exactly one slot; every other slot holds 240, meaning empty.
All inputs are finite; a program needn't handle non-finite values.
Results may differ from a plain program's by a relative error of at most 0.008.
Values may be sent and summed in bfloat16 or wider, within the bound.
A program may use at most 192 MiB of HBM per device.

v0:
```python
import functools

import jax
import jax.numpy as jnp
from jax import lax
from jax.experimental import pallas as pl
from jax.experimental.pallas import tpu as pltpu
from jax.sharding import PartitionSpec as P


SPREADS = (1.85, 2.55, 3.3)
VMEM_LIMIT = 60 * 1024 * 1024
LANES = 128


def recurrence_kernel(unroll, where_ref, upper_ref, lower_ref, order_ref, cosine_ref, start_ref, out_ref):
    degree_range = upper_ref.shape[0]
    latitude_count = out_ref.shape[2]
    pieces = [(lo, min(lo + LANES, latitude_count)) for lo in range(0, latitude_count, LANES)]
    out_ref[...] = jnp.zeros_like(out_ref)
    order = order_ref[...]
    cosine = [cosine_ref[:, lo:hi] for lo, hi in pieces]
    start = [start_ref[:, lo:hi] for lo, hi in pieces]

    def body(step, carry):
        latest, before = carry
        for inner in range(unroll):
            level = step * unroll + inner
            row = where_ref[level]
            upper = upper_ref[level]
            lower = lower_ref[level]
            begins = order == level
            fresh = []
            for i, (lo, hi) in enumerate(pieces):
                width = hi - lo
                grown = upper[:, :width] * (cosine[i] * latest[i] - lower[:, :width] * before[i])
                value = jnp.where(begins[:, :width], start[i], grown)
                out_ref[row, :, lo:hi] = value.astype(jnp.bfloat16)
                fresh.append(value)
            latest, before = fresh, latest
        return latest, before

    zeros = [jnp.zeros_like(c) for c in cosine]
    lax.fori_loop(0, degree_range // unroll, body, (zeros, zeros))


def picked_legendre(orders, degree_table, degree_range, latitude_count):
    slots = orders.shape[0]
    total = degree_table.shape[0]
    order_real = orders.astype(jnp.float32)[:, None]
    angles = jnp.pi * (jnp.arange(latitude_count).astype(jnp.float32) + 0.5) / latitude_count
    cosine = jnp.cos(angles)[None, :]
    sine = jnp.sin(angles)[None, :]
    counter = jnp.arange(1, degree_range + 1).astype(jnp.float32)
    factors = jnp.log((2.0 * counter - 1.0) / (2.0 * counter))
    below = (counter[None, :] <= order_real).astype(jnp.float32)
    log_start = 0.5 * (
        jnp.log((2.0 * order_real + 1.0) / (4.0 * jnp.pi))
        + jnp.sum(below * factors[None, :], axis=1, keepdims=True)
    )
    parity = 1.0 - 2.0 * (orders % 2).astype(jnp.float32)[:, None]
    start = parity * jnp.exp(log_start + order_real * jnp.log(sine))

    level = jnp.arange(degree_range).astype(jnp.float32)[:, None]
    order_wide = order_real[:, 0][None, :]
    upper = jnp.sqrt(
        jnp.maximum(4.0 * level * level - 1.0, 0.0)
        / jnp.maximum(level * level - order_wide * order_wide, 1.0)
    )
    lower = jnp.sqrt(
        jnp.maximum((level - 1.0) * (level - 1.0) - order_wide * order_wide, 0.0)
        / jnp.maximum(4.0 * (level - 1.0) * (level - 1.0) - 1.0, 1.0)
    )
    upper, lower = (
        jnp.broadcast_to(lax.optimization_barrier(part)[:, :, None], part.shape + (LANES,))
        for part in (upper, lower)
    )
    places = jnp.arange(total).astype(jnp.int32)
    degrees = jnp.arange(degree_range).astype(jnp.int32)
    where = jnp.sum(
        jnp.where(degree_table[None, :] == degrees[:, None], places[None, :], 0), axis=1
    )
    where = jnp.minimum(where, total - 1).astype(jnp.int32)
    unroll = next(u for u in (8, 6, 5, 4, 3, 2, 1) if degree_range % u == 0)
    vmem = pl.BlockSpec(memory_space=pltpu.VMEM)
    return pl.pallas_call(
        functools.partial(recurrence_kernel, unroll),
        out_shape=jax.ShapeDtypeStruct((total, slots, latitude_count), jnp.bfloat16),
        in_specs=[pl.BlockSpec(memory_space=pltpu.SMEM)] + [vmem] * 5,
        out_specs=vmem,
        cost_estimate=pl.CostEstimate(
            flops=6 * degree_range * slots * latitude_count,
            bytes_accessed=24 * 1024 * 1024,
            transcendentals=0,
        ),
        name="legendre",
    )(
        where,
        upper,
        lower,
        jnp.broadcast_to(orders[:, None], (slots, LANES)),
        jnp.broadcast_to(cosine, (slots, latitude_count)),
        start,
    )


def quadrature(latitude_count):
    angles = jnp.pi * (jnp.arange(latitude_count).astype(jnp.float32) + 0.5) / latitude_count
    return jnp.pi / latitude_count * jnp.sin(angles)


def exchange(value):
    return lax.all_to_all(value, "order", split_axis=0, concat_axis=0, tiled=True)


def pack(packer, value):
    return jnp.einsum(
        "tpks,tksc->tpc", packer, value, preferred_element_type=jnp.float32
    ).astype(jnp.bfloat16)


def swap(value, bit):
    count = lax.axis_size("chan")
    return lax.ppermute(value, "chan", [(i, i ^ bit) for i in range(count)])


def gather_channels(value):
    count = lax.axis_size("chan")
    if count & (count - 1):
        whole = lax.all_gather(value, "chan", axis=0)
        return [whole[i] for i in range(count)], jnp.arange(count).astype(jnp.int32)
    blocks, flips = [value], [0]
    bit = count // 2
    while bit:
        blocks = blocks + [swap(block, bit) for block in blocks]
        flips = flips + [flip ^ bit for flip in flips]
        bit //= 2
    owners = jnp.bitwise_xor(lax.axis_index("chan"), jnp.array(flips, jnp.int32))
    return blocks, owners


def window_rows(plan_ref, peers, step, window):
    base = step * peers * 3
    spans = []
    for p in range(peers):
        where = pl.multiple_of(plan_ref[base + 3 * p], 16)
        spans.append((pl.ds(where, window), plan_ref[base + 3 * p + 1], plan_ref[base + 3 * p + 2]))
    return spans


def coefficient_kernel(peers, window, blocks, plan_ref, owner_ref, *refs):
    gathered, (weight_ref, out_ref) = refs[:blocks], refs[blocks:]
    step = pl.program_id(0)
    width = out_ref.shape[2]

    @pl.when(step == 0)
    def _():
        out_ref[...] = jnp.zeros_like(out_ref)

    spans = window_rows(plan_ref, peers, step, window)
    total = None
    for b, ref in enumerate(gathered):
        rows = jnp.concatenate([ref[p, span, :] for p, (span, _, _) in enumerate(spans)], axis=0)
        lanes = pl.ds(pl.multiple_of(owner_ref[b] * width, width), width)
        part = lax.dot_general(
            rows, weight_ref[0, :, lanes], (((1,), (1,)), ((), ())), preferred_element_type=jnp.float32
        )
        total = part if total is None else total + part
    index = lax.broadcasted_iota(jnp.int32, (window, width), 0)
    for p, (span, first, _) in enumerate(spans):
        kept = out_ref[p, span, :].astype(jnp.float32)
        fresh = total[p * window : (p + 1) * window]
        out_ref[p, span, :] = jnp.where(index >= first, fresh, kept).astype(jnp.bfloat16)


def mixing_kernel(peers, window, blocks, rows_of, plan_ref, owner_ref, *refs):
    gathered = [refs[r * blocks : (r + 1) * blocks] for r in range(rows_of)]
    saved = refs[rows_of * blocks : rows_of * (blocks + 1)]
    out_ref = refs[-1]
    step = pl.program_id(0)
    width = saved[0].shape[2]
    spans = window_rows(plan_ref, peers, step, window)
    index = lax.broadcasted_iota(jnp.int32, (window, width), 0)
    masked = []
    for r in range(rows_of):
        for p, (span, first, last) in enumerate(spans):
            value = saved[r][p, span, :].astype(jnp.float32)
            inside = (index >= first) & (index < last)
            masked.append(jnp.where(inside, value, 0.0).astype(jnp.bfloat16))
    left = jnp.concatenate(masked, axis=0)
    for b in range(blocks):
        right = jnp.concatenate(
            [gathered[r][b][p, span, :] for r in range(rows_of) for p, (span, _, _) in enumerate(spans)],
            axis=0,
        )
        lanes = pl.ds(pl.multiple_of(owner_ref[b] * width, width), width)
        out_ref[0, :, lanes] = lax.dot_general(
            left, right, (((0,), (0,)), ((), ())), preferred_element_type=jnp.float32
        ).astype(jnp.bfloat16)


def whole_block(shape):
    return pl.BlockSpec(shape, lambda k, *_: (0,) * len(shape), pipeline_mode=pl.Buffered(1))


def coefficients(plan, owners, window, gathered, weights):
    slots, width, channels = weights.shape
    peers = gathered[0].shape[0]
    kernel = functools.partial(coefficient_kernel, peers, window, len(gathered))
    return pl.pallas_call(
        kernel,
        grid_spec=pltpu.PrefetchScalarGridSpec(
            num_scalar_prefetch=2,
            grid=(slots,),
            in_specs=[whole_block(part.shape) for part in gathered]
            + [pl.BlockSpec((1, width, channels), lambda k, *_: (k, 0, 0))],
            out_specs=whole_block(gathered[0].shape),
        ),
        out_shape=jax.ShapeDtypeStruct(gathered[0].shape, jnp.bfloat16),
        compiler_params=pltpu.CompilerParams(vmem_limit_bytes=VMEM_LIMIT),
        cost_estimate=pl.CostEstimate(
            flops=2 * slots * peers * window * width * channels,
            bytes_accessed=2 * (weights.size + (len(gathered) + 1) * gathered[0].size),
            transcendentals=0,
        ),
        name="coefficients",
    )(plan, owners, *gathered, weights)


def mixing_gradients(plan, owners, window, gathered, saved, slots):
    rows_of, blocks = len(gathered), len(gathered[0])
    peers, _, width = saved[0].shape
    operands = [part for parts in gathered for part in parts] + list(saved)
    return pl.pallas_call(
        functools.partial(mixing_kernel, peers, window, blocks, rows_of),
        grid_spec=pltpu.PrefetchScalarGridSpec(
            num_scalar_prefetch=2,
            grid=(slots,),
            in_specs=[whole_block(part.shape) for part in operands],
            out_specs=pl.BlockSpec((1, width, width * blocks), lambda k, *_: (k, 0, 0)),
        ),
        out_shape=jax.ShapeDtypeStruct((slots, width, width * blocks), jnp.bfloat16),
        compiler_params=pltpu.CompilerParams(vmem_limit_bytes=VMEM_LIMIT),
        cost_estimate=pl.CostEstimate(
            flops=2 * slots * peers * window * rows_of * width * width * blocks,
            bytes_accessed=2 * (slots * width * width * blocks + len(operands) * saved[0].size),
            transcendentals=0,
        ),
        name="mixing",
    )(plan, owners, *operands)


def layer(capacity, *operands):
    return layer_body(capacity, *operands)


def layer_body(
    capacity, cotangent, stored_coefficients, weights, order_table, degree_table, mine, owned
):
    slots, latitude_count, batch_size, parts, width = cotangent.shape
    degree_range = stored_coefficients.shape[1]
    peers = lax.axis_size("order")
    full = slots * slots
    rows = batch_size * parts
    cot = cotangent.reshape(slots, latitude_count, rows, width)
    stored = stored_coefficients.reshape(slots, degree_range, rows, width)
    degrees = jnp.arange(degree_range).astype(jnp.int32)

    valid = (degree_table[:, None] >= mine[None, :]) & (degree_table[:, None] < degree_range)
    flags = valid.reshape(peers, full).astype(jnp.bfloat16)
    index = jnp.arange(full)
    before = (index[:, None] < index[None, :]).astype(jnp.bfloat16)
    rank = jnp.dot(flags, before, preferred_element_type=jnp.float32).astype(jnp.int32)
    rank = jnp.where(valid.reshape(peers, full), rank, -1).reshape(peers, slots, slots)
    place = jnp.arange(capacity).astype(jnp.int32)[None, :, None, None]
    packer = (rank[:, None] == place).astype(jnp.bfloat16)

    window = min(-(-slots // 16) * 16 + 16, capacity)
    lengths = jnp.sum(
        (
            (order_table.reshape(peers, slots)[None] <= owned[:, None, None])
            & (owned[:, None, None] < degree_range)
        ).astype(jnp.int32),
        axis=2,
    )
    steps = jnp.arange(slots)
    earlier = (steps[:, None] > steps[None, :]).astype(jnp.int32)
    offsets = jnp.sum(earlier[:, :, None] * lengths[None], axis=1)
    starts = jnp.minimum(offsets // 16 * 16, capacity - window)
    first = offsets - starts
    plan = jnp.stack([starts, first, first + lengths], axis=2).reshape(-1).astype(jnp.int32)

    pick = (degree_table[:, None, None] == degrees[None, None, :]) & valid[:, :, None]
    pick = pick.astype(jnp.bfloat16).reshape(peers, slots, slots, degree_range)

    def project(matrix, source):
        return jnp.einsum(
            "tksj,sjc->tksc", matrix, source, preferred_element_type=jnp.float32
        ).astype(jnp.bfloat16)

    def send_saved(r):
        return exchange(pack(packer, project(pick, stored[:, :, r])))

    def send_adjoint(r):
        moved = exchange(pack(packer, project(table, cot[:, :, r])))
        return gather_channels(moved)

    saved = [send_saved(0)]
    table = picked_legendre(mine, degree_table, degree_range, latitude_count)
    table = table.reshape(peers, slots, slots, latitude_count)
    gathered = []
    for r in range(rows):
        blocks, owners = send_adjoint(r)
        gathered.append(blocks)
    saved += [send_saved(r) for r in range(1, rows)]
    quad = quadrature(latitude_count)
    outputs = []
    for r in range(rows):
        coefficient = coefficients(plan, owners, window, gathered[r], weights)
        moved = exchange(coefficient)
        returned = jnp.einsum(
            "tpks,tpc->tksc", packer, moved, preferred_element_type=jnp.float32
        ).astype(jnp.bfloat16)
        summed = jnp.einsum("tksj,tksc->sjc", table, returned, preferred_element_type=jnp.float32)
        outputs.append((summed * quad[None, :, None]).astype(jnp.bfloat16))
    mixing_gradient = mixing_gradients(plan, owners, window, gathered, saved, slots)
    return jnp.stack(outputs, axis=2).reshape(cotangent.shape), mixing_gradient


def capacities(slots, peers, degree_range):
    full = slots * slots
    live = degree_range * (degree_range + 1) / 2 / (peers * slots) ** 2
    spread = (full * (2 * slots + 1) / 12) ** 0.5
    most = -(-full // 16) * 16
    steps = [-(-int(live * full + s * spread) // 16) * 16 for s in SPREADS]
    return [c for c in steps if c <= 0.85 * most] + [most]


def per_device(cotangent, stored_coefficients, weights, order_table, degree_table):
    slots = cotangent.shape[0]
    degree_range = stored_coefficients.shape[1]
    peers = lax.axis_size("order")
    position = lax.axis_index("order")
    mine = lax.dynamic_slice_in_dim(order_table, position * slots, slots)
    owned = lax.dynamic_slice_in_dim(degree_table, position * slots, slots)
    operands = (cotangent, stored_coefficients, weights, order_table, degree_table, mine, owned)
    tiers = capacities(slots, peers, degree_range)
    if len(tiers) == 1:
        return layer_body(tiers[0], *operands)
    order_rows = order_table.reshape(peers, 1, slots, 1)
    degree_rows = degree_table.reshape(1, peers, 1, slots)
    counts = jnp.sum(
        ((degree_rows >= order_rows) & (degree_rows < degree_range)).astype(jnp.int32), axis=(2, 3)
    )
    most = jnp.max(counts)
    tier = sum((most > c).astype(jnp.int32) for c in tiers[:-1])
    return lax.switch(tier, [functools.partial(layer, c) for c in tiers], *operands)


def solution(mesh):
    return jax.shard_map(
        per_device,
        mesh=mesh,
        in_specs=(
            P("order", None, None, None, "chan"),
            P("order", None, None, None, "chan"),
            P("order", "chan", None),
            P(),
            P(),
        ),
        out_specs=(P("order", None, None, None, "chan"), P("order", "chan", None)),
        check_vma=False,
    )
```

profile of v0, /device:TPU:0, one launch (start us, length us, event | category | flops | bytes accessed | tf_op | source)
XLA Modules:
  0.0 504.9 jit_solution(1359952242307053889)
XLA Ops:
  0.6 0.8 ge.137
  1.4 0.8 ge.139
  2.2 0.5 convert_reduce_fusion.4
  2.7 0.6 reduce_max.9
  5.3 496.2 %conditional.1 = (bf16[31,256,1024]{2,1,0:T(8,128)(2,1)}, bf16[31,240,1,2,256]{4,3,2,1,0:T(2,128)(2,1)S(1)}) conditional(s32[]{:T(128)} %clamp.3, (s32[248]{0:T(256)}, s32[248]{0:T(256)}, s32[248]{0:T(256)}, s32[248]{0:T(256)}, (), /*index=5*/bf16[31,240,1,2,256]{4,3,2,1,0:T(2,128)(2,1)}, ...), branch_computations={%region_2.7_spmd, %region_7.12_spmd, %region_12.17_spmd, %region_1... | conditional | flops 53778788352 | bytes 614731712 | solution.py:357
  13.6 0.8 select_reduce_fusion.4
  14.4 0.8 ge.114
  15.1 0.7 broadcast_compare_fusion.4
  15.8 0.8 fusion.272
  16.6 0.2 select_reduce_fusion.5
  17.1 0.6 broadcast_minimum_fusion.2.where_ref
  17.7 7.4 %copy.457 = bf16[31,240,1,2,256]{4,1,0,3,2:T(8,128)(2,1)} copy(bf16[31,240,1,2,256]{4,3,2,1,0:T(2,128)(2,1)} %get-tuple-element.301) | data formatting | bytes 15237120 | tf_op jit(solution)/shard_map
  25.8 0.3 fusion.250
  26.1 0.2 eq.172
  26.3 0.7 exponential_multiply_fusion.2.start_ref
  26.9 2.5 broadcast_in_dim.113.upper_ref
  29.4 2.5 broadcast_in_dim.114.lower_ref
  31.9 0.7 broadcast_in_dim.115.order_ref
  32.6 0.6 broadcast_in_dim.116.cosine_ref
  33.2 7.5 %legendre.6 = bf16[248,31,240]{2,1,0:T(8,128)(2,1)} custom-call(s32[240]{0:T(256)} %broadcast_minimum_fusion.2.where_ref, f32[240,31,128]{2,1,0:T(8,128)} %broadcast_in_dim.113.upper_ref, f32[240,31,128]{2,1,0:T(8,128)} %broadcast_in_dim.114.lower_ref, s32[31,128]{1,0:T(8,128)} %broadcast_in_dim.115.order_ref, f32[31,240]{1,0:T(8,128)} %broadcast_in_dim.116.cosine_ref, ...), custom_call_target="tpu_custom_call" | custom-call | flops 10713600 | bytes 25165824 | tf_op jit(solution)/shard_map/cond/branch_2_fun/legendre/pallas_call | solution.py:86
  40.7 7.9 %convert_bitcast_fusion.11 = bf16[8,31,31,256]{3,1,0,2:T(8,128)(2,1)S(1)} fusion(bf16[31,240,2,256]{3,1,0,2:T(8,128)(2,1)} %bitcast.450, bf16[8,31,31,240]{3,2,1,0:T(8,128)(2,1)} %bitcast.474), kind=kOutput, calls=%fused_computation.281 | convolution fusion | flops 946669568 | bytes 11808768 | tf_op jit(solution)/shard_map/cond/branch_2_fun/tksj,sjc->tksc/dot_general | solution.py:297
  48.6 10.1 %bitcast_convert_fusion.11 = bf16[8,688,256]{2,1,0:T(8,128)(2,1)} fusion(bf16[8,31,31,256]{3,1,0,2:T(8,128)(2,1)S(1)} %convert_bitcast_fusion.11, s32[8,31,31]{2,1,0:T(8,128)S(1)} %eq.172), kind=kOutput, calls=%fused_computation.269 | convolution fusion | flops 2714842624 | bytes 6785056 | tf_op jit(solution)/shard_map/cond/branch_2_fun/tpks,tksc->tpc/dot_general | solution.py:117
  58.7 7.5 %all-to-all-start = ((bf16[8,688,256]{2,1,0:T(8,128)(2,1)}), bf16[8,688,256]{2,1,0:T(8,128)(2,1)S(1)}, u32[]{:S(2)}, u32[]{:S(2)}) async-start(bf16[8,688,256]{2,1,0:T(8,128)(2,1)} %bitcast_convert_fusion.11), calls=%async_computation | async-start | bytes 5636096 | tf_op jit(solution)/shard_map/cond/branch_2_fun/all_to_all | solution.py:113
  66.2 7.9 %convert_bitcast_fusion.10 = bf16[8,31,31,256]{3,1,0,2:T(8,128)(2,1)S(1)} fusion(bf16[31,240,2,256]{3,1,0,2:T(8,128)(2,1)} %bitcast.451, bf16[8,31,31,240]{3,2,1,0:T(8,128)(2,1)} %bitcast.475), kind=kOutput, calls=%fused_computation.278 | convolution fusion | flops 946669568 | bytes 11808768 | tf_op jit(solution)/shard_map/cond/branch_2_fun/tksj,sjc->tksc/dot_general | solution.py:297
  74.1 10.2 %bitcast_convert_fusion.10 = bf16[8,688,256]{2,1,0:T(8,128)(2,1)} fusion(bf16[8,31,31,256]{3,1,0,2:T(8,128)(2,1)S(1)} %convert_bitcast_fusion.10, s32[8,31,31]{2,1,0:T(8,128)S(1)} %eq.172), kind=kOutput, calls=%fused_computation.268 | convolution fusion | flops 2714842624 | bytes 6785056 | tf_op jit(solution)/shard_map/cond/branch_2_fun/tpks,tksc->tpc/dot_general | solution.py:117
  84.3 45.6 %all-to-all-done.refs_0_ = bf16[8,688,256]{2,1,0:T(8,128)(2,1)S(1)} async-done(((bf16[8,688,256]{2,1,0:T(8,128)(2,1)}), bf16[8,688,256]{2,1,0:T(8,128)(2,1)S(1)}, u32[]{:S(2)}, u32[]{:S(2)}) %all-to-all-start) | async-done | bytes 2818080 | tf_op jit(solution)/shard_map/cond/branch_2_fun/all_to_all | solution.py:113
  129.9 4.4 all-to-all-start.2
  134.4 0.2 copy.239
  134.6 4.3 copy.456
  139.0 2.0 convert_bitcast_fusion.9
  141.1 1.0 copy-done.6
  142.0 10.1 %bitcast_convert_fusion.9 = bf16[8,688,256]{2,1,0:T(8,128)(2,1)} fusion(bf16[8,31,31,256]{3,1,0,2:T(8,128)(2,1)S(1)} %convert_bitcast_fusion.9, s32[8,31,31]{2,1,0:T(8,128)S(1)} %eq.172), kind=kOutput, calls=%fused_computation.267 | convolution fusion | flops 2714842624 | bytes 6785056 | tf_op jit(solution)/shard_map/cond/branch_2_fun/tpks,tksc->tpc/dot_general | solution.py:117
  152.1 45.4 %all-to-all-done.2.refs_0_.refs_4_ = bf16[8,688,256]{2,1,0:T(8,128)(2,1)} async-done(((bf16[8,688,256]{2,1,0:T(8,128)(2,1)}), bf16[8,688,256]{2,1,0:T(8,128)(2,1)}, u32[]{:S(2)}, u32[]{:S(2)}) %all-to-all-start.2) | async-done | bytes 2818080 | tf_op jit(solution)/shard_map/cond/branch_2_fun/all_to_all | solution.py:113
  197.5 4.8 all-to-all-start.4
  202.3 3.9 convert_bitcast_fusion.8
  206.2 1.6 collective-permute-start
  207.8 10.1 %bitcast_convert_fusion.8 = bf16[8,688,256]{2,1,0:T(8,128)(2,1)} fusion(bf16[8,31,31,256]{3,1,0,2:T(8,128)(2,1)S(1)} %convert_bitcast_fusion.8, s32[8,31,31]{2,1,0:T(8,128)S(1)} %eq.172), kind=kOutput, calls=%fused_computation.266 | convolution fusion | flops 2714842624 | bytes 6785056 | tf_op jit(solution)/shard_map/cond/branch_2_fun/tpks,tksc->tpc/dot_general | solution.py:117
  217.8 47.7 %all-to-all-done.4.refs_8_ = bf16[8,688,256]{2,1,0:T(8,128)(2,1)} async-done(((bf16[8,688,256]{2,1,0:T(8,128)(2,1)}), bf16[8,688,256]{2,1,0:T(8,128)(2,1)}, u32[]{:S(2)}, u32[]{:S(2)}) %all-to-all-start.4) | async-done | bytes 2818080 | tf_op jit(solution)/shard_map/cond/branch_2_fun/all_to_all | solution.py:113
  265.5 4.4 all-to-all-start.5
  270.0 0.5 collective-permute-start.2
  270.7 0.7 convert_reduce_fusion.2
  271.4 1.6 collective-permute-start.3
  273.1 0.6 multiply_reduce_fusion.2
  273.8 0.2 copy.230
  273.9 0.8 reshape.1082.plan_ref
  274.7 0.6 broadcast_xor_fusion.2.owner_ref
  275.3 4.0 collective-permute-done.2.refs_3_
  279.4 29.8 %coefficients.12 = bf16[8,688,256]{2,1,0:T(8,128)(2,1)} custom-call(s32[744]{0:T(1024)} %reshape.1082.plan_ref, s32[4]{0:T(128)} %broadcast_xor_fusion.2.owner_ref, bf16[8,688,256]{2,1,0:T(8,128)(2,1)} %copy-done.1, bf16[8,688,256]{2,1,0:T(8,128)(2,1)} %collective-permute-done.refs_1_, bf16[8,688,256]{2,1,0:T(8,128)(2,1)} %collective-permute-done.1.refs_2_, ...), custom_call_target="tpu_custom_call" | custom-call | flops 6241124352 | bytes 30343168 | tf_op jit(solution)/shard_map/cond/branch_2_fun/coefficients/pallas_call | solution.py:210
  309.2 23.9 %all-to-all-done.5.refs_9_ = bf16[8,688,256]{2,1,0:T(8,128)(2,1)} async-done(((bf16[8,688,256]{2,1,0:T(8,128)(2,1)}), bf16[8,688,256]{2,1,0:T(8,128)(2,1)}, u32[]{:S(2)}, u32[]{:S(2)}) %all-to-all-start.5) | async-done | bytes 2818080 | tf_op jit(solution)/shard_map/cond/branch_2_fun/all_to_all | solution.py:113
  333.1 3.6 all-to-all-start.1
  336.8 0.5 collective-permute-start.5
  337.3 5.0 collective-permute-done.4.refs_2_.refs_6_
  342.4 4.0 collective-permute-done.5.refs_3_.refs_7_
  346.4 29.8 %coefficients.13 = bf16[8,688,256]{2,1,0:T(8,128)(2,1)} custom-call(s32[744]{0:T(1024)} %reshape.1082.plan_ref, s32[4]{0:T(128)} %broadcast_xor_fusion.2.owner_ref, bf16[8,688,256]{2,1,0:T(8,128)(2,1)} %all-to-all-done.2.refs_0_.refs_4_, bf16[8,688,256]{2,1,0:T(8,128)(2,1)} %collective-permute-done.3.refs_1_.refs_5_, ...), custom_call_target="tpu_custom_call" | custom-call | flops 6241124352 | bytes 30343168 | tf_op jit(solution)/shard_map/cond/branch_2_fun/coefficients/pallas_call | solution.py:210
  376.2 24.4 %all-to-all-done.1 = bf16[8,688,256]{2,1,0:T(8,128)(2,1)S(1)} async-done(((bf16[8,688,256]{2,1,0:T(8,128)(2,1)}), bf16[8,688,256]{2,1,0:T(8,128)(2,1)S(1)}, u32[]{:S(2)}, u32[]{:S(2)}) %all-to-all-start.1) | async-done | bytes 2818080 | tf_op jit(solution)/shard_map/cond/branch_2_fun/all_to_all | solution.py:113
  400.6 4.5 all-to-all-start.3
  405.1 5.6 %iota_compare_fusion.44 = pred[8,688,31,31]{1,3,2,0:T(8,128)(4,1)} fusion(s32[8,31,31]{2,1,0:T(8,128)S(1)} %eq.172), kind=kLoop, calls=%fused_computation.242 | loop fusion | flops 5289344 | bytes 5320096 | tf_op jit(solution)/shard_map/cond/branch_2_fun/eq | solution.py:276
  410.7 33.0 %mixing.6 = bf16[31,256,1024]{2,1,0:T(8,128)(2,1)} custom-call(s32[744]{0:T(1024)} %reshape.1082.plan_ref, s32[4]{0:T(128)} %broadcast_xor_fusion.2.owner_ref, bf16[8,688,256]{2,1,0:T(8,128)(2,1)} %copy-done.1, bf16[8,688,256]{2,1,0:T(8,128)(2,1)} %collective-permute-done.refs_1_, bf16[8,688,256]{2,1,0:T(8,128)(2,1)} %collective-permute-done.1.refs_2_, ...), custom_call_target="tpu_custom_call" | custom-call | flops 12482248704 | bytes 44433408 | tf_op jit(solution)/shard_map/cond/branch_2_fun/mixing/pallas_call | solution.py:234
  443.7 11.5 %fusion.203 = bf16[31,240,1,256]{3,1,0,2:T(8,128)(2,1)} fusion(f32[240]{0:T(256)S(1)} %fusion.268, bf16[8,31,31,240]{3,2,1,0:T(8,128)(2,1)} %bitcast.476, pred[8,688,31,31]{1,3,2,0:T(8,128)(4,1)} %iota_compare_fusion.44, bf16[8,688,256]{2,1,0:T(8,128)(2,1)S(1)} %all-to-all-done.1), kind=kOutput, calls=%fused_computation.288 | convolution fusion | flops 3658622976 | bytes 15607872 | tf_op jit(solution)/shard_map/cond/branch_2_fun/tksj,tksc->sjc/dot_general | solution.py:324
  455.2 13.0 %all-to-all-done.3 = bf16[8,688,256]{2,1,0:T(8,128)(2,1)} async-done(((bf16[8,688,256]{2,1,0:T(8,128)(2,1)}), bf16[8,688,256]{2,1,0:T(8,128)(2,1)}, u32[]{:S(2)}, u32[]{:S(2)}) %all-to-all-start.3) | async-done | bytes 2818080 | tf_op jit(solution)/shard_map/cond/branch_2_fun/all_to_all | solution.py:113
  468.2 12.2 %fusion.204 = bf16[31,240,1,256]{3,1,0,2:T(8,128)(2,1)} fusion(f32[240]{0:T(256)S(1)} %fusion.268, bf16[8,31,31,240]{3,2,1,0:T(8,128)(2,1)} %bitcast.477, pred[8,688,31,31]{1,3,2,0:T(8,128)(4,1)} %iota_compare_fusion.44, bf16[8,688,256]{2,1,0:T(8,128)(2,1)} %all-to-all-done.3), kind=kOutput, calls=%fused_computation.289 | convolution fusion | flops 3658622976 | bytes 15607872 | tf_op jit(solution)/shard_map/cond/branch_2_fun/tksj,tksc->sjc/dot_general | solution.py:324
  480.5 3.9 maximum_bitcast_fusion.2
  484.4 10.1 %copy.310 = bf16[31,240,1,2,256]{4,3,2,1,0:T(2,128)(2,1)S(1)} copy(bf16[31,240,1,2,256]{4,1,0,3,2:T(8,128)(2,1)S(1)} %maximum_bitcast_fusion.2) | data formatting | bytes 15237120 | tf_op jit(solution)/shard_map/cond | solution.py:357
  501.5 3.1 copy-done.8
  (44 shorter events, 1.9 us)
Async XLA Ops:
  58.7 71.1 %all-to-all-start = ((bf16[8,688,256]{2,1,0:T(8,128)(2,1)}), bf16[8,688,256]{2,1,0:T(8,128)(2,1)S(1)}, u32[]{:S(2)}, u32[]{:S(2)}) async-start(bf16[8,688,256]{2,1,0:T(8,128)(2,1)} %bitcast_convert_fusion.11), calls=%async_computation | async-start | bytes 5636096 | tf_op jit(solution)/shard_map/cond/branch_2_fun/all_to_all | solution.py:113
  129.8 140.1 %copy-start.1 = (bf16[8,688,256]{2,1,0:T(8,128)(2,1)}, bf16[8,688,256]{2,1,0:T(8,128)(2,1)S(1)}, u32[]{:S(2)}) copy-start(bf16[8,688,256]{2,1,0:T(8,128)(2,1)S(1)} %all-to-all-done.refs_0_) | copy-start | bytes 8454148 | tf_op jit(solution)/shard_map/cond
  129.9 67.6 %all-to-all-start.2 = ((bf16[8,688,256]{2,1,0:T(8,128)(2,1)}), bf16[8,688,256]{2,1,0:T(8,128)(2,1)}, u32[]{:S(2)}, u32[]{:S(2)}) async-start(bf16[8,688,256]{2,1,0:T(8,128)(2,1)} %bitcast_convert_fusion.10), calls=%async_computation.2 | async-start | bytes 5636096 | tf_op jit(solution)/shard_map/cond/branch_2_fun/all_to_all | solution.py:113
  138.9 3.1 copy-start.6
  197.5 68.0 %all-to-all-start.4 = ((bf16[8,688,256]{2,1,0:T(8,128)(2,1)}), bf16[8,688,256]{2,1,0:T(8,128)(2,1)}, u32[]{:S(2)}, u32[]{:S(2)}) async-start(bf16[8,688,256]{2,1,0:T(8,128)(2,1)} %bitcast_convert_fusion.9), calls=%async_computation.4 | async-start | bytes 5636096 | tf_op jit(solution)/shard_map/cond/branch_2_fun/all_to_all | solution.py:113
  206.2 63.9 %collective-permute-start = (bf16[8,688,256]{2,1,0:T(8,128)(2,1)S(1)}, bf16[8,688,256]{2,1,0:T(8,128)(2,1)}, u32[]{:S(2)}, u32[]{:S(2)}) collective-permute-start(bf16[8,688,256]{2,1,0:T(8,128)(2,1)S(1)} %all-to-all-done.refs_0_), channel_id=1, source_target_pairs={{0,2},{1,3},{2,0},{3,1},{4,6},{5,7},{6,4},{7,5},{8,10},{9,11},{10,... | collective-permute-start | bytes 8454152 | tf_op jit(solution)/shard_map/cond/branch_2_fun/ppermute | solution.py:124
  217.8 52.7 %copy-start.24 = (s32[248]{0:T(256)S(1)}, s32[248]{0:T(256)}, u32[]{:S(2)}) copy-start(s32[248]{0:T(256)} %get-tuple-element.82) | copy-start | bytes 2980 | tf_op jit(solution)/shard_map/cond
  217.8 52.8 %copy-start.20 = (s32[248]{0:T(256)S(1)}, s32[248]{0:T(256)}, u32[]{:S(2)}) copy-start(s32[248]{0:T(256)} %get-tuple-element.112) | copy-start | bytes 2980 | tf_op jit(solution)/shard_map/cond
  217.8 56.9 %copy-start.28 = (s32[4]{0:T(128)S(1)}, s32[4]{0:T(128)}, u32[]{:S(2)}) copy-start(s32[4]{0:T(128)} %constant.323.clone.3) | copy-start | bytes 52 | tf_op jit(solution)/shard_map/cond
  265.5 67.6 %all-to-all-start.5 = ((bf16[8,688,256]{2,1,0:T(8,128)(2,1)}), bf16[8,688,256]{2,1,0:T(8,128)(2,1)}, u32[]{:S(2)}, u32[]{:S(2)}) async-start(bf16[8,688,256]{2,1,0:T(8,128)(2,1)} %bitcast_convert_fusion.8), calls=%async_computation.5 | async-start | bytes 5636096 | tf_op jit(solution)/shard_map/cond/branch_2_fun/all_to_all | solution.py:113
  269.9 5.4 %collective-permute-start.1 = (bf16[8,688,256]{2,1,0:T(8,128)(2,1)S(1)}, bf16[8,688,256]{2,1,0:T(8,128)(2,1)}, u32[]{:S(2)}, u32[]{:S(2)}) collective-permute-start(bf16[8,688,256]{2,1,0:T(8,128)(2,1)S(1)} %all-to-all-done.refs_0_), channel_id=1, source_target_pairs={{0,1},{1,0},{2,3},{3,2},{4,5},{5,4},{6,7},{7,6},{8,9},{9,8},{10,11... | collective-permute-start | bytes 8454152 | tf_op jit(solution)/shard_map/cond/branch_2_fun/ppermute | solution.py:124
  270.0 9.3 %collective-permute-start.2 = (bf16[8,688,256]{2,1,0:T(8,128)(2,1)}, bf16[8,688,256]{2,1,0:T(8,128)(2,1)}, u32[]{:S(2)}, u32[]{:S(2)}) collective-permute-start(bf16[8,688,256]{2,1,0:T(8,128)(2,1)} %collective-permute-done.refs_1_), channel_id=1, source_target_pairs={{0,1},{1,0},{2,3},{3,2},{4,5},{5,4},{6,7},{7,6},{8,9},{9,8},{10,11... | collective-permute-start | bytes 8454152 | tf_op jit(solution)/shard_map/cond/branch_2_fun/ppermute | solution.py:124
  271.4 65.4 %collective-permute-start.3 = (bf16[8,688,256]{2,1,0:T(8,128)(2,1)}, bf16[8,688,256]{2,1,0:T(8,128)(2,1)}, u32[]{:S(2)}, u32[]{:S(2)}) collective-permute-start(bf16[8,688,256]{2,1,0:T(8,128)(2,1)} %all-to-all-done.2.refs_0_.refs_4_), channel_id=1, source_target_pairs={{0,2},{1,3},{2,0},{3,1},{4,6},{5,7},{6,4},{7,5},{8,10},{9,11},{10,... | collective-permute-start | bytes 8454152 | tf_op jit(solution)/shard_map/cond/branch_2_fun/ppermute | solution.py:124
  333.1 67.5 %all-to-all-start.1 = ((bf16[8,688,256]{2,1,0:T(8,128)(2,1)}), bf16[8,688,256]{2,1,0:T(8,128)(2,1)S(1)}, u32[]{:S(2)}, u32[]{:S(2)}) async-start(bf16[8,688,256]{2,1,0:T(8,128)(2,1)} %coefficients.12), calls=%async_computation.1 | async-start | bytes 5636096 | tf_op jit(solution)/shard_map/cond/branch_2_fun/all_to_all | solution.py:113
  336.8 5.6 %collective-permute-start.4 = (bf16[8,688,256]{2,1,0:T(8,128)(2,1)}, bf16[8,688,256]{2,1,0:T(8,128)(2,1)}, u32[]{:S(2)}, u32[]{:S(2)}) collective-permute-start(bf16[8,688,256]{2,1,0:T(8,128)(2,1)} %all-to-all-done.2.refs_0_.refs_4_), channel_id=1, source_target_pairs={{0,1},{1,0},{2,3},{3,2},{4,5},{5,4},{6,7},{7,6},{8,9},{9,8},{10,11... | collective-permute-start | bytes 8454152 | tf_op jit(solution)/shard_map/cond/branch_2_fun/ppermute | solution.py:124
  336.8 9.5 %collective-permute-start.5 = (bf16[8,688,256]{2,1,0:T(8,128)(2,1)}, bf16[8,688,256]{2,1,0:T(8,128)(2,1)}, u32[]{:S(2)}, u32[]{:S(2)}) collective-permute-start(bf16[8,688,256]{2,1,0:T(8,128)(2,1)} %collective-permute-done.3.refs_1_.refs_5_), channel_id=1, source_target_pairs={{0,1},{1,0},{2,3},{3,2},{4,5},{5,4},{6,7},{7,6},{8,9},{9,8},{10,11... | collective-permute-start | bytes 8454152 | tf_op jit(solution)/shard_map/cond/branch_2_fun/ppermute | solution.py:124
  400.6 67.6 %all-to-all-start.3 = ((bf16[8,688,256]{2,1,0:T(8,128)(2,1)}), bf16[8,688,256]{2,1,0:T(8,128)(2,1)}, u32[]{:S(2)}, u32[]{:S(2)}) async-start(bf16[8,688,256]{2,1,0:T(8,128)(2,1)} %coefficients.13), calls=%async_computation.3 | async-start | bytes 5636096 | tf_op jit(solution)/shard_map/cond/branch_2_fun/all_to_all | solution.py:113
  501.5 3.1 copy-start.8
where the time goes:
time: 515 us; the launch traced here: 505 us
  waiting for transfers between devices  213 us (41%)
  Pallas kernels  100 us (19%)
  matrix products  86.2 us (17%)
  local copies, waits for them, and re-layouts  36.9 us (7%)
  starting transfers between devices  33.5 us (7%)
  other arithmetic  17 us (3%)
  loops' own time  15.4 us (3%)
    all_to_all x6, waiting for transfers between devices, exchange(): lax.all_to_all(value, 'order', split_axis=0, concat_axis=0, tiled=True)  200 us
    pallas_call x2, Pallas kernels, coefficients(): pl.pallas_call(kernel, grid_spec=pltpu.PrefetchScalarGridSpec(num_scalar_...  59.6 us
    dot_general x4, matrix products, pack(): jnp.einsum('tpks,tksc->tpc', packer, value, preferred_element_type=jnp.fl...  40.5 us
    pallas_call x1, Pallas kernels, mixing_gradients(): pl.pallas_call(functools.partial(mixing_kernel, peers, window, blocks, ro...  33 us
    all_to_all x6, starting transfers between devices, exchange(): lax.all_to_all(value, 'order', split_axis=0, concat_axis=0, tiled=True)  29.3 us
    dot_general x2, matrix products, layer_body(): jnp.einsum('tksj,tksc->sjc', table, returned, preferred_element_type=jnp....  23.7 us
    dot_general x4, matrix products, project(): jnp.einsum('tksj,sjc->tksc', matrix, source, preferred_element_type=jnp.f...  21.7 us
    another operation x1, loops' own time, per_device(): lax.switch(tier, [functools.partial(layer, c) for c in tiers], *operands)  15.4 us
  transfers between devices with their start and end apart: 12, of which 9 were waited for; matrix products, arithmetic and copies ran while one was open for 14% of the time, Pallas kernels for 18%

commit v1 on v0

--- a/solution.py
+++ b/solution.py
@@ -8,7 +8,7 @@
 from jax.sharding import PartitionSpec as P
 
 
-SPREADS = (1.85, 2.55, 3.3)
+SPREADS = (2.1, 2.8, 3.5)
 VMEM_LIMIT = 60 * 1024 * 1024
 LANES = 128
 
@@ -117,6 +117,44 @@
     return jnp.einsum(
         "tpks,tksc->tpc", packer, value, preferred_element_type=jnp.float32
     ).astype(jnp.bfloat16)
+
+
+def final_kernel(others, table_ref, value_ref, quad_ref, *refs):
+    earlier, out_ref = refs[:others], refs[others]
+    batch, count = table_ref.shape[:2]
+    for i in range(batch):
+        values = value_ref[i].reshape(count, value_ref.shape[-1])
+        summed = lax.dot_general(
+            table_ref[i], values, (((0,), (0,)), ((), ())), preferred_element_type=jnp.float32
+        )
+        parts = [ref[i].astype(jnp.float32) for ref in earlier] + [summed * quad_ref[...]]
+        out_ref[i] = jnp.stack(parts, axis=1).astype(jnp.bfloat16)
+
+
+def final_rows(table, values, quad, earlier):
+    slots, count, latitude_count = table.shape
+    peers, padded, width = values.shape[1:]
+    batch = min(4, slots)
+    parts = len(earlier) + 1
+    return pl.pallas_call(
+        functools.partial(final_kernel, len(earlier)),
+        grid=(-(-slots // batch),),
+        in_specs=[
+            pl.BlockSpec((batch, count, latitude_count), lambda i: (i, 0, 0)),
+            pl.BlockSpec((batch, peers, padded, width), lambda i: (i, 0, 0, 0)),
+            pl.BlockSpec(quad.shape, lambda i: (0, 0)),
+        ]
+        + [pl.BlockSpec((batch, latitude_count, width), lambda i: (i, 0, 0))] * len(earlier),
+        out_specs=pl.BlockSpec((batch, latitude_count, parts, width), lambda i: (i, 0, 0, 0)),
+        out_shape=jax.ShapeDtypeStruct((slots, latitude_count, parts, width), jnp.bfloat16),
+        compiler_params=pltpu.CompilerParams(vmem_limit_bytes=VMEM_LIMIT),
+        cost_estimate=pl.CostEstimate(
+            flops=2 * table.size * width,
+            bytes_accessed=2 * (table.size + values.size + 2 * parts * slots * latitude_count * width),
+            transcendentals=0,
+        ),
+        name="final",
+    )(table, values, quad, *earlier)
 
 
 def swap(value, bit):
@@ -275,6 +313,11 @@
     place = jnp.arange(capacity).astype(jnp.int32)[None, :, None, None]
     packer = (rank[:, None] == place).astype(jnp.bfloat16)
 
+    padded = -(-slots // 16) * 16
+    spare = padded - slots
+    wide = jnp.pad(rank, ((0, 0), (0, spare), (0, 0)), constant_values=-1)
+    wide_packer = (wide[:, None] == place).astype(jnp.bfloat16)
+
     window = min(-(-slots // 16) * 16 + 16, capacity)
     lengths = jnp.sum(
         (
@@ -308,6 +351,8 @@
     saved = [send_saved(0)]
     table = picked_legendre(mine, degree_table, degree_range, latitude_count)
     table = table.reshape(peers, slots, slots, latitude_count)
+    turned = jnp.pad(table, ((0, 0), (0, spare), (0, 0), (0, 0))).transpose(2, 0, 1, 3)
+    turned = turned.reshape(slots, peers * padded, latitude_count)
     gathered = []
     for r in range(rows):
         blocks, owners = send_adjoint(r)
@@ -318,13 +363,23 @@
     for r in range(rows):
         coefficient = coefficients(plan, owners, window, gathered[r], weights)
         moved = exchange(coefficient)
+        form = "tpks,tpc->tksc" if r < rows - 1 else "tpks,tpc->stkc"
         returned = jnp.einsum(
-            "tpks,tpc->tksc", packer, moved, preferred_element_type=jnp.float32
+            form,
+            packer if r < rows - 1 else wide_packer,
+            moved,
+            preferred_element_type=jnp.float32,
         ).astype(jnp.bfloat16)
-        summed = jnp.einsum("tksj,tksc->sjc", table, returned, preferred_element_type=jnp.float32)
-        outputs.append((summed * quad[None, :, None]).astype(jnp.bfloat16))
+        if r < rows - 1:
+            summed = jnp.einsum(
+                "tksj,tksc->sjc", table, returned, preferred_element_type=jnp.float32
+            )
+            outputs.append((summed * quad[None, :, None]).astype(jnp.bfloat16))
+        else:
+            spread = jnp.broadcast_to(quad[:, None], (latitude_count, width))
+            outputs = final_rows(turned, returned, spread, outputs)
     mixing_gradient = mixing_gradients(plan, owners, window, gathered, saved, slots)
-    return jnp.stack(outputs, axis=2).reshape(cotangent.shape), mixing_gradient
+    return outputs.reshape(cotangent.shape), mixing_gradient
 
 
 def capacities(slots, peers, degree_range):
@@ -334,6 +389,13 @@
     most = -(-full // 16) * 16
     steps = [-(-int(live * full + s * spread) // 16) * 16 for s in SPREADS]
     return [c for c in steps if c <= 0.85 * most] + [most]
+
+
+def choose(tier, tiers, operands):
+    first = functools.partial(layer, tiers[0])
+    if len(tiers) == 1:
+        return first(*operands)
+    return lax.cond(tier == 0, first, lambda *rest: choose(tier - 1, tiers[1:], rest), *operands)
 
 
 def per_device(cotangent, stored_coefficients, weights, order_table, degree_table):
@@ -354,7 +416,7 @@
     )
     most = jnp.max(counts)
     tier = sum((most > c).astype(jnp.int32) for c in tiers[:-1])
-    return lax.switch(tier, [functools.partial(layer, c) for c in tiers], *operands)
+    return choose(tier, tiers, operands)
 
 
 def solution(mesh):

time: 515 us -> 546 us (1.060)
  loops' own time: 15.4 us -> 39 us
  Pallas kernels: 100 us -> 117 us
  other arithmetic: 17 us -> 10.8 us
  waiting for transfers between devices: 213 us -> 219 us
    another operation x1 -> x3, loops' own time: 15.4 us -> 39 us  [choose(): lax.cond(tier == 0, first, lambda *rest: choose(tier - 1, tiers[1:], rest...]
    pallas_call x0 -> x1, Pallas kernels: none -> 16.7 us  [final_rows(): pl.pallas_call(functools.partial(final_kernel, len(earlier)), grid=(-(-sl...]
    dot_general x2 -> x1, matrix products: 23.7 us -> 11.4 us  [layer_body(): jnp.einsum('tksj,tksc->sjc', table, returned, preferred_element_type=jnp....]
    cond x11 -> x21, local copies, waits for them, and re-layouts: 11.1 us -> 1.72 us  [the longest x1 10.1 us: per_device(): lax.switch(tier, [functools.partial(layer, c) for c in tiers], *operands)]
    dot_general x0 -> x1, matrix products: none -> 7.81 us  [layer_body(): jnp.einsum(form, packer if r < rows - 1 else wide_packer, moved, preferre...]
    all_to_all x6, waiting for transfers between devices: 200 us -> 207 us  [exchange(): lax.all_to_all(value, 'order', split_axis=0, concat_axis=0, tiled=True)]
  transfers between devices with their start and end apart: 12 -> 12, of which waited for: 9 -> 10; matrix products, arithmetic and copies ran while one was open for 14% -> 13% of each run, Pallas kernels for 18% -> 17%
where the time goes in v1:
time: 546 us; the launch traced here: 541 us
  waiting for transfers between devices  219 us (40%)
  Pallas kernels  117 us (21%)
  matrix products  83.5 us (15%)
  loops' own time  39 us (7%)
  local copies, waits for them, and re-layouts  34.1 us (6%)
  starting transfers between devices  33.8 us (6%)
  other arithmetic  10.8 us (2%)
    all_to_all x6, waiting for transfers between devices, exchange(): lax.all_to_all(value, 'order', split_axis=0, concat_axis=0, tiled=True)  207 us
    pallas_call x2, Pallas kernels, coefficients(): pl.pallas_call(kernel, grid_spec=pltpu.PrefetchScalarGridSpec(num_scalar_...  59.7 us
    dot_general x4, matrix products, pack(): jnp.einsum('tpks,tksc->tpc', packer, value, preferred_element_type=jnp.fl...  40.5 us
    another operation x3, loops' own time, choose(): lax.cond(tier == 0, first, lambda *rest: choose(tier - 1, tiers[1:], rest...  39 us
    pallas_call x1, Pallas kernels, mixing_gradients(): pl.pallas_call(functools.partial(mixing_kernel, peers, window, blocks, ro...  33.1 us
    all_to_all x6, starting transfers between devices, exchange(): lax.all_to_all(value, 'order', split_axis=0, concat_axis=0, tiled=True)  29.5 us
    dot_general x4, matrix products, project(): jnp.einsum('tksj,sjc->tksc', matrix, source, preferred_element_type=jnp.f...  23.5 us
    pallas_call x1, Pallas kernels, final_rows(): pl.pallas_call(functools.partial(final_kernel, len(earlier)), grid=(-(-sl...  16.7 us
  transfers between devices with their start and end apart: 12, of which 10 were waited for; matrix products, arithmetic and copies ran while one was open for 13% of the time, Pallas kernels for 17%

profile of v1, /device:TPU:0, one launch (start us, length us, event | category | flops | bytes accessed | tf_op | source)
XLA Modules:
  0.0 541.0 jit_solution(8120863185388249232)
XLA Ops:
  0.6 0.8 ge.137
  1.4 0.8 ge.139
  2.2 0.5 convert_reduce_fusion.4
  2.7 0.6 reduce_max.9
  5.3 0.8 dynamic_slice.6
  6.0 1.3 dynamic_slice.7
  7.3 532.5 %conditional.3 = ((bf16[31,240,1,2,256]{4,3,1,0,2:T(2,128)(2,1)}, bf16[31,256,1024]{2,1,0:T(8,128)(2,1)})) conditional(s32[]{:T(128)} %convert_element_type.550, (s32[]{:T(128)}, s32[248]{0:T(256)}, s32[31]{0:T(128)S(1)}, s32[248]{0:T(256)}, s32[31]{0:T(128)}, /*index=5*/s32[4]{0:T(128)}, bf16[31,240,1,2,256]{4,3,2,1,0:T(2,128)(2,1)}, ...), branch_computations={%region_2.19_spmd, %region_19.24_spmd} | conditional | flops 53937319936 | bytes 543548800 | solution.py:398
  7.3 7.5 %copy.255 = bf16[31,240,1,2,256]{4,1,0,3,2:T(8,128)(2,1)} copy(bf16[31,240,1,2,256]{4,3,2,1,0:T(2,128)(2,1)} %get-tuple-element.236) | data formatting | bytes 15237120 | tf_op jit(solution)/shard_map
  14.9 4.2 copy.256
  19.0 504.6 %conditional.1 = ((bf16[31,240,1,2,256]{4,3,1,0,2:T(2,128)(2,1)}, bf16[31,256,1024]{2,1,0:T(8,128)(2,1)})) conditional(s32[]{:T(128)} %convert_element_type.509, (s32[]{:T(128)}, s32[248]{0:T(256)S(1)}, s32[31]{0:T(128)S(1)}, s32[248]{0:T(256)}, s32[31]{0:T(128)}, /*index=5*/s32[4]{0:T(128)}, bf16[31,240,1,2,256]{4,1,0,3,2:T(8,128)(2,1)}, ...), branch_computations={%region_3.13_spmd, %region_14.18_spmd} | conditional | flops 53937319936 | bytes 490214688 | solution.py:398
  19.0 489.3 %conditional = (bf16[31,240,1,2,256]{4,3,1,0,2:T(2,128)(2,1)}, bf16[31,256,1024]{2,1,0:T(8,128)(2,1)}) conditional(s32[]{:T(128)} %convert_element_type.477, (s32[248]{0:T(256)S(1)}, s32[31]{0:T(128)S(1)}, s32[248]{0:T(256)}, s32[31]{0:T(128)}, s32[4]{0:T(128)}, /*index=5*/bf16[31,240,1,2,256]{4,1,0,3,2:T(8,128)(2,1)}, ...), branch_computations={%region_4.7_spmd, %region_9.12_spmd} | conditional | flops 53937319936 | bytes 490214528 | solution.py:398
  26.4 0.2 select_reduce_fusion.3
  26.9 0.6 broadcast_minimum_fusion.1.where_ref
  28.2 0.3 fusion.137
  28.5 0.2 eq.182
  28.6 0.7 exponential_multiply_fusion.1.start_ref
  29.3 2.5 broadcast_in_dim.115.upper_ref
  31.8 2.5 broadcast_in_dim.116.lower_ref
  34.3 0.7 broadcast_in_dim.117.order_ref
  35.0 0.6 broadcast_in_dim.118.cosine_ref
  35.6 7.5 %legendre.5 = bf16[248,31,240]{2,1,0:T(8,128)(2,1)} custom-call(s32[240]{0:T(256)} %broadcast_minimum_fusion.1.where_ref, f32[240,31,128]{2,1,0:T(8,128)} %broadcast_in_dim.115.upper_ref, f32[240,31,128]{2,1,0:T(8,128)} %broadcast_in_dim.116.lower_ref, s32[31,128]{1,0:T(8,128)} %broadcast_in_dim.117.order_ref, f32[31,240]{1,0:T(8,128)} %broadcast_in_dim.118.cosine_ref, ...), custom_call_target="tpu_custom_call" | custom-call | flops 10713600 | bytes 25165824 | tf_op jit(solution)/shard_map/cond/branch_0_fun/cond/branch_0_fun/cond/branch_1_fun/legendre/pallas_call | solution.py:86
  43.1 7.9 %convert_bitcast_fusion.7 = bf16[8,31,31,256]{3,1,0,2:T(8,128)(2,1)S(1)} fusion(bf16[31,240,2,256]{3,1,0,2:T(8,128)(2,1)} %bitcast.433, bf16[8,31,31,240]{3,2,1,0:T(8,128)(2,1)} %bitcast.410), kind=kOutput, calls=%fused_computation.145 | convolution fusion | flops 946669568 | bytes 11808768 | tf_op jit(solution)/shard_map/cond/branch_0_fun/cond/branch_0_fun/cond/branch_1_fun/tksj,sjc->tksc/dot_general | solution.py:340
  51.0 10.2 %bitcast_convert_fusion.6 = bf16[8,704,256]{2,1,0:T(8,128)(2,1)} fusion(bf16[8,31,31,256]{3,1,0,2:T(8,128)(2,1)S(1)} %convert_bitcast_fusion.7, s32[8,31,31]{2,1,0:T(8,128)S(1)} %eq.182), kind=kOutput, calls=%fused_computation.135 | convolution fusion | flops 2777978368 | bytes 6850592 | tf_op jit(solution)/shard_map/cond/branch_0_fun/cond/branch_0_fun/cond/branch_1_fun/tpks,tksc->tpc/dot_general | solution.py:117
  61.1 7.7 %all-to-all-start.8 = ((bf16[8,704,256]{2,1,0:T(8,128)(2,1)}), bf16[8,704,256]{2,1,0:T(8,128)(2,1)S(1)}, u32[]{:S(2)}, u32[]{:S(2)}) async-start(bf16[8,704,256]{2,1,0:T(8,128)(2,1)} %bitcast_convert_fusion.6), calls=%async_computation.8 | async-start | bytes 5767168 | tf_op jit(solution)/shard_map/cond/branch_0_fun/cond/branch_0_fun/cond/branch_1_fun/all_to_all | solution.py:113
  68.8 7.9 %convert_bitcast_fusion.9 = bf16[8,31,31,256]{3,1,0,2:T(8,128)(2,1)S(1)} fusion(bf16[31,240,2,256]{3,1,0,2:T(8,128)(2,1)} %bitcast.434, bf16[8,31,31,240]{3,2,1,0:T(8,128)(2,1)} %bitcast.411), kind=kOutput, calls=%fused_computation.147 | convolution fusion | flops 946669568 | bytes 11808768 | tf_op jit(solution)/shard_map/cond/branch_0_fun/cond/branch_0_fun/cond/branch_1_fun/tksj,sjc->tksc/dot_general | solution.py:340
  76.7 10.2 %bitcast_convert_fusion.7 = bf16[8,704,256]{2,1,0:T(8,128)(2,1)} fusion(bf16[8,31,31,256]{3,1,0,2:T(8,128)(2,1)S(1)} %convert_bitcast_fusion.9, s32[8,31,31]{2,1,0:T(8,128)S(1)} %eq.182), kind=kOutput, calls=%fused_computation.136 | convolution fusion | flops 2777978368 | bytes 6850592 | tf_op jit(solution)/shard_map/cond/branch_0_fun/cond/branch_0_fun/cond/branch_1_fun/tpks,tksc->tpc/dot_general | solution.py:117
  86.9 47.0 %all-to-all-done.8.refs_0_ = bf16[8,704,256]{2,1,0:T(8,128)(2,1)S(1)} async-done(((bf16[8,704,256]{2,1,0:T(8,128)(2,1)}), bf16[8,704,256]{2,1,0:T(8,128)(2,1)S(1)}, u32[]{:S(2)}, u32[]{:S(2)}) %all-to-all-start.8) | async-done | bytes 2883616 | tf_op jit(solution)/shard_map/cond/branch_0_fun/cond/branch_0_fun/cond/branch_1_fun/all_to_all | solution.py:113
  133.9 4.4 all-to-all-start.6
  138.7 3.9 convert_bitcast_fusion.6
  142.6 10.1 %bitcast_convert_fusion.5 = bf16[8,704,256]{2,1,0:T(8,128)(2,1)} fusion(bf16[8,31,31,256]{3,1,0,2:T(8,128)(2,1)S(1)} %convert_bitcast_fusion.6, s32[8,31,31]{2,1,0:T(8,128)S(1)} %eq.182), kind=kOutput, calls=%fused_computation.134 | convolution fusion | flops 2777978368 | bytes 6850592 | tf_op jit(solution)/shard_map/cond/branch_0_fun/cond/branch_0_fun/cond/branch_1_fun/tpks,tksc->tpc/dot_general | solution.py:117
  152.7 50.2 %all-to-all-done.6.refs_0_.refs_4_ = bf16[8,704,256]{2,1,0:T(8,128)(2,1)} async-done(((bf16[8,704,256]{2,1,0:T(8,128)(2,1)}), bf16[8,704,256]{2,1,0:T(8,128)(2,1)}, u32[]{:S(2)}, u32[]{:S(2)}) %all-to-all-start.6) | async-done | bytes 2883616 | tf_op jit(solution)/shard_map/cond/branch_0_fun/cond/branch_0_fun/cond/branch_1_fun/all_to_all | solution.py:113
  202.9 4.6 all-to-all-start.10
  207.5 3.9 convert_bitcast_fusion.5
  211.4 1.6 collective-permute-start.6
  213.0 10.1 %bitcast_convert_fusion.4 = bf16[8,704,256]{2,1,0:T(8,128)(2,1)} fusion(bf16[8,31,31,256]{3,1,0,2:T(8,128)(2,1)S(1)} %convert_bitcast_fusion.5, s32[8,31,31]{2,1,0:T(8,128)S(1)} %eq.182), kind=kOutput, calls=%fused_computation.133 | convolution fusion | flops 2777978368 | bytes 6850592 | tf_op jit(solution)/shard_map/cond/branch_0_fun/cond/branch_0_fun/cond/branch_1_fun/tpks,tksc->tpc/dot_general | solution.py:117
  223.1 49.0 %all-to-all-done.10.refs_8_ = bf16[8,704,256]{2,1,0:T(8,128)(2,1)} async-done(((bf16[8,704,256]{2,1,0:T(8,128)(2,1)}), bf16[8,704,256]{2,1,0:T(8,128)(2,1)}, u32[]{:S(2)}, u32[]{:S(2)}) %all-to-all-start.10) | async-done | bytes 2883616 | tf_op jit(solution)/shard_map/cond/branch_0_fun/cond/branch_0_fun/cond/branch_1_fun/all_to_all | solution.py:113
  272.1 4.4 all-to-all-start.11
  276.6 0.5 collective-permute-start.8
  277.2 0.7 convert_reduce_fusion.1
  277.9 1.6 collective-permute-start.9
  279.6 0.6 multiply_reduce_fusion.1
  280.5 0.8 reshape.1119.plan_ref
  281.3 0.6 broadcast_xor_fusion.1.owner_ref
  281.8 0.4 collective-permute-done.7.refs_2_.refs_6_
  282.2 4.1 collective-permute-done.8.refs_3_.refs_7_
  286.4 29.9 %coefficients.10 = bf16[8,704,256]{2,1,0:T(8,128)(2,1)} custom-call(s32[744]{0:T(1024)} %reshape.1119.plan_ref, s32[4]{0:T(128)} %broadcast_xor_fusion.1.owner_ref, bf16[8,704,256]{2,1,0:T(8,128)(2,1)} %all-to-all-done.6.refs_0_.refs_4_, bf16[8,704,256]{2,1,0:T(8,128)(2,1)} %collective-permute-done.6.refs_1_.refs_5_, ...), custom_call_target="tpu_custom_call" | custom-call | flops 6241124352 | bytes 30670848 | tf_op jit(solution)/shard_map/cond/branch_0_fun/cond/branch_0_fun/cond/branch_1_fun/coefficients/pallas_call | solution.py:248
  316.2 24.9 %all-to-all-done.11.refs_9_ = bf16[8,704,256]{2,1,0:T(8,128)(2,1)} async-done(((bf16[8,704,256]{2,1,0:T(8,128)(2,1)}), bf16[8,704,256]{2,1,0:T(8,128)(2,1)}, u32[]{:S(2)}, u32[]{:S(2)}) %all-to-all-start.11) | async-done | bytes 2883616 | tf_op jit(solution)/shard_map/cond/branch_0_fun/cond/branch_0_fun/cond/branch_1_fun/all_to_all | solution.py:113
  341.1 4.4 all-to-all-start.7
  345.7 0.5 collective-permute-start.11
  346.2 4.8 collective-permute-done.10.refs_2_
  350.9 1.5 copy-done.6
  352.5 2.7 collective-permute-done.11.refs_3_
  355.2 29.8 %coefficients.11 = bf16[8,704,256]{2,1,0:T(8,128)(2,1)} custom-call(s32[744]{0:T(1024)} %reshape.1119.plan_ref, s32[4]{0:T(128)} %broadcast_xor_fusion.1.owner_ref, bf16[8,704,256]{2,1,0:T(8,128)(2,1)} %copy-done.2, bf16[8,704,256]{2,1,0:T(8,128)(2,1)} %collective-permute-done.9.refs_1_, bf16[8,704,256]{2,1,0:T(8,128)(2,1)} %copy-done.6, ...), custom_call_target="tpu_custom_call" | custom-call | flops 6241124352 | bytes 30670848 | tf_op jit(solution)/shard_map/cond/branch_0_fun/cond/branch_0_fun/cond/branch_1_fun/coefficients/pallas_call | solution.py:248
  385.0 25.1 %all-to-all-done.7 = bf16[8,704,256]{2,1,0:T(8,128)(2,1)} async-done(((bf16[8,704,256]{2,1,0:T(8,128)(2,1)}), bf16[8,704,256]{2,1,0:T(8,128)(2,1)}, u32[]{:S(2)}, u32[]{:S(2)}) %all-to-all-start.7) | async-done | bytes 2883616 | tf_op jit(solution)/shard_map/cond/branch_0_fun/cond/branch_0_fun/cond/branch_1_fun/all_to_all | solution.py:113
  410.1 3.9 all-to-all-start.9
  414.2 4.5 copy.203
  418.6 3.2 pad.20
  421.8 5.6 %iota_compare_fusion.24 = pred[8,704,31,31]{1,3,2,0:T(8,128)(4,1)} fusion(s32[8,31,31]{2,1,0:T(8,128)S(1)} %eq.182), kind=kLoop, calls=%fused_computation.114 | loop fusion | flops 5412352 | bytes 5443104 | tf_op jit(solution)/shard_map/cond/branch_0_fun/cond/branch_0_fun/cond/branch_1_fun/eq | solution.py:314
  427.4 33.1 %mixing.5 = bf16[31,256,1024]{2,1,0:T(8,128)(2,1)} custom-call(s32[744]{0:T(1024)} %reshape.1119.plan_ref, s32[4]{0:T(128)} %broadcast_xor_fusion.1.owner_ref, bf16[8,704,256]{2,1,0:T(8,128)(2,1)} %copy-done.2, bf16[8,704,256]{2,1,0:T(8,128)(2,1)} %collective-permute-done.9.refs_1_, bf16[8,704,256]{2,1,0:T(8,128)(2,1)} %copy-done.6, ...), custom_call_target="tpu_custom_call" | custom-call | flops 12482248704 | bytes 45088768 | tf_op jit(solution)/shard_map/cond/branch_0_fun/cond/branch_0_fun/cond/branch_1_fun/mixing/pallas_call | solution.py:272
  460.6 7.8 %convert_bitcast_fusion.8.value_ref = bf16[31,8,32,256]{3,2,1,0:T(8,128)(2,1)} fusion(bf16[8,704,256]{2,1,0:T(8,128)(2,1)} %all-to-all-done.7, s32[8,32,31]{1,2,0:T(8,128)S(1)} %pad.21.clone), kind=kOutput, calls=%fused_computation.146 | convolution fusion | flops 2868133888 | bytes 6978560 | tf_op jit(solution)/shard_map/cond/branch_0_fun/cond/branch_0_fun/cond/branch_1_fun/tpks,tpc->stkc/dot_general | solution.py:367
  468.4 10.8 %all-to-all-done.9 = bf16[8,704,256]{2,1,0:T(8,128)(2,1)S(1)} async-done(((bf16[8,704,256]{2,1,0:T(8,128)(2,1)}), bf16[8,704,256]{2,1,0:T(8,128)(2,1)S(1)}, u32[]{:S(2)}, u32[]{:S(2)}) %all-to-all-start.9) | async-done | bytes 2883616 | tf_op jit(solution)/shard_map/cond/branch_0_fun/cond/branch_0_fun/cond/branch_1_fun/all_to_all | solution.py:113
  479.2 11.4 %fusion.102.refs_0_ = bf16[31,240,256]{2,1,0:T(8,128)(2,1)} fusion(f32[240]{0:T(256)S(1)} %fusion.155, bf16[8,31,31,240]{3,2,1,0:T(8,128)(2,1)} %bitcast.413, pred[8,704,31,31]{1,3,2,0:T(8,128)(4,1)} %iota_compare_fusion.24, bf16[8,704,256]{2,1,0:T(8,128)(2,1)S(1)} %all-to-all-done.9), kind=kOutput, calls=%fused_computation.132 | convolution fusion | flops 3721603072 | bytes 15796416 | tf_op jit(solution)/shard_map/cond/branch_0_fun/cond/branch_0_fun/cond/branch_1_fun/tksj,tksc->sjc/dot_general | solution.py:374
  490.6 0.8 broadcast_in_dim.120.quad_ref
  491.4 16.7 %final.5 = bf16[31,240,2,256]{3,2,1,0:T(2,128)(2,1)} custom-call(bf16[31,256,240]{2,1,0:T(8,128)(2,1)} %bitcast.424, bf16[31,8,32,256]{3,2,1,0:T(8,128)(2,1)} %convert_bitcast_fusion.8.value_ref, f32[240,256]{1,0:T(8,128)} %broadcast_in_dim.120.quad_ref, bf16[31,240,256]{2,1,0:T(8,128)(2,1)} %fusion.102.refs_0_), custom_call_target="tpu_custom_call" | custom-call | flops 975175680 | bytes 23109632 | tf_op jit(solution)/shard_map/cond/branch_0_fun/cond/branch_0_fun/cond/branch_1_fun/final/pallas_call | solution.py:139
  (60 shorter events, 2.5 us)
Async XLA Ops:
  7.3 7.5 %slice-start = ((s8[7618560]{0:T(1024)(128)(4,1)}), s8[4194304]{0:T(1024)(128)(4,1)S(1)}, s32[]{:S(2)}) async-start(s8[7618560]{0:T(1024)(128)(4,1)} %bitcast.404), calls=%async_computation.24 | async-start | bytes 8388608 | tf_op jit(solution)/shard_map/cond
  7.3 7.5 %slice-start.1 = ((s8[7618560]{0:T(1024)(128)(4,1)}), s8[3424256]{0:T(1024)(128)(4,1)S(1)}, s32[]{:S(2)}) async-start(s8[7618560]{0:T(1024)(128)(4,1)} %bitcast.404), calls=%async_computation.25 | async-start | bytes 6848512 | tf_op jit(solution)/shard_map/cond
  14.8 4.2 copy-start.14
  26.0 8.3 %copy-start.8 = (s32[31]{0:T(128)}, s32[31]{0:T(128)S(1)}, u32[]{:S(2)}) copy-start(s32[31]{0:T(128)S(1)} %get-tuple-element.115) | copy-start | bytes 376 | tf_op jit(solution)/shard_map/cond/branch_0_fun/cond/branch_0_fun/cond
  61.1 72.8 %all-to-all-start.8 = ((bf16[8,704,256]{2,1,0:T(8,128)(2,1)}), bf16[8,704,256]{2,1,0:T(8,128)(2,1)S(1)}, u32[]{:S(2)}, u32[]{:S(2)}) async-start(bf16[8,704,256]{2,1,0:T(8,128)(2,1)} %bitcast_convert_fusion.6), calls=%async_computation.8 | async-start | bytes 5767168 | tf_op jit(solution)/shard_map/cond/branch_0_fun/cond/branch_0_fun/cond/branch_1_fun/all_to_all | solution.py:113
  86.9 51.4 %copy-start.9 = (s32[31]{0:T(128)S(1)}, s32[31]{0:T(128)}, u32[]{:S(2)}) copy-start(s32[31]{0:T(128)} %copy-done.8) | copy-start | bytes 376 | tf_op jit(solution)/shard_map/cond/branch_0_fun/cond/branch_0_fun/cond
  133.9 211.7 %copy-start.2 = (bf16[8,704,256]{2,1,0:T(8,128)(2,1)}, bf16[8,704,256]{2,1,0:T(8,128)(2,1)S(1)}, u32[]{:S(2)}) copy-start(bf16[8,704,256]{2,1,0:T(8,128)(2,1)S(1)} %all-to-all-done.8.refs_0_) | copy-start | bytes 8650756 | tf_op jit(solution)/shard_map/cond/branch_0_fun/cond/branch_0_fun/cond
  133.9 69.0 %all-to-all-start.6 = ((bf16[8,704,256]{2,1,0:T(8,128)(2,1)}), bf16[8,704,256]{2,1,0:T(8,128)(2,1)}, u32[]{:S(2)}, u32[]{:S(2)}) async-start(bf16[8,704,256]{2,1,0:T(8,128)(2,1)} %bitcast_convert_fusion.7), calls=%async_computation.6 | async-start | bytes 5767168 | tf_op jit(solution)/shard_map/cond/branch_0_fun/cond/branch_0_fun/cond/branch_1_fun/all_to_all | solution.py:113
  202.9 69.2 %all-to-all-start.10 = ((bf16[8,704,256]{2,1,0:T(8,128)(2,1)}), bf16[8,704,256]{2,1,0:T(8,128)(2,1)}, u32[]{:S(2)}, u32[]{:S(2)}) async-start(bf16[8,704,256]{2,1,0:T(8,128)(2,1)} %bitcast_convert_fusion.5), calls=%async_computation.10 | async-start | bytes 5767168 | tf_op jit(solution)/shard_map/cond/branch_0_fun/cond/branch_0_fun/cond/branch_1_fun/all_to_all | solution.py:113
  211.4 65.2 %collective-permute-start.6 = (bf16[8,704,256]{2,1,0:T(8,128)(2,1)}, bf16[8,704,256]{2,1,0:T(8,128)(2,1)}, u32[]{:S(2)}, u32[]{:S(2)}) collective-permute-start(bf16[8,704,256]{2,1,0:T(8,128)(2,1)} %all-to-all-done.6.refs_0_.refs_4_), channel_id=1, source_target_pairs={{0,2},{1,3},{2,0},{3,1},{4,6},{5,7},{6,4},{7,5},{8,10},{9,11},{10,... | collective-permute-start | bytes 8650760 | tf_op jit(solution)/shard_map/cond/branch_0_fun/cond/branch_0_fun/cond/branch_1_fun/ppermute | solution.py:162
  223.1 54.0 %copy-start.16 = (s32[248]{0:T(256)S(1)}, s32[248]{0:T(256)}, u32[]{:S(2)}) copy-start(s32[248]{0:T(256)} %get-tuple-element.116) | copy-start | bytes 2980 | tf_op jit(solution)/shard_map/cond/branch_0_fun/cond/branch_0_fun/cond
  223.1 54.1 %copy-start.20 = (s32[31]{0:T(128)S(1)}, s32[31]{0:T(128)}, u32[]{:S(2)}) copy-start(s32[31]{0:T(128)} %get-tuple-element.117) | copy-start | bytes 376 | tf_op jit(solution)/shard_map/cond/branch_0_fun/cond/branch_0_fun/cond
  223.1 58.1 %copy-start.24 = (s32[4]{0:T(128)S(1)}, s32[4]{0:T(128)}, u32[]{:S(2)}) copy-start(s32[4]{0:T(128)} %get-tuple-element.118) | copy-start | bytes 52 | tf_op jit(solution)/shard_map/cond/branch_0_fun/cond/branch_0_fun/cond
  272.1 69.0 %all-to-all-start.11 = ((bf16[8,704,256]{2,1,0:T(8,128)(2,1)}), bf16[8,704,256]{2,1,0:T(8,128)(2,1)}, u32[]{:S(2)}, u32[]{:S(2)}) async-start(bf16[8,704,256]{2,1,0:T(8,128)(2,1)} %bitcast_convert_fusion.4), calls=%async_computation.11 | async-start | bytes 5767168 | tf_op jit(solution)/shard_map/cond/branch_0_fun/cond/branch_0_fun/cond/branch_1_fun/all_to_all | solution.py:113
  276.5 5.7 %collective-permute-start.7 = (bf16[8,704,256]{2,1,0:T(8,128)(2,1)}, bf16[8,704,256]{2,1,0:T(8,128)(2,1)}, u32[]{:S(2)}, u32[]{:S(2)}) collective-permute-start(bf16[8,704,256]{2,1,0:T(8,128)(2,1)} %all-to-all-done.6.refs_0_.refs_4_), channel_id=1, source_target_pairs={{0,1},{1,0},{2,3},{3,2},{4,5},{5,4},{6,7},{7,6},{8,9},{9,8},{10,11... | collective-permute-start | bytes 8650760 | tf_op jit(solution)/shard_map/cond/branch_0_fun/cond/branch_0_fun/cond/branch_1_fun/ppermute | solution.py:162
  276.6 9.7 %collective-permute-start.8 = (bf16[8,704,256]{2,1,0:T(8,128)(2,1)}, bf16[8,704,256]{2,1,0:T(8,128)(2,1)}, u32[]{:S(2)}, u32[]{:S(2)}) collective-permute-start(bf16[8,704,256]{2,1,0:T(8,128)(2,1)} %collective-permute-done.6.refs_1_.refs_5_), channel_id=1, source_target_pairs={{0,1},{1,0},{2,3},{3,2},{4,5},{5,4},{6,7},{7,6},{8,9},{9,8},{10,11... | collective-permute-start | bytes 8650760 | tf_op jit(solution)/shard_map/cond/branch_0_fun/cond/branch_0_fun/cond/branch_1_fun/ppermute | solution.py:162
  277.9 67.7 %collective-permute-start.9 = (bf16[8,704,256]{2,1,0:T(8,128)(2,1)S(1)}, bf16[8,704,256]{2,1,0:T(8,128)(2,1)}, u32[]{:S(2)}, u32[]{:S(2)}) collective-permute-start(bf16[8,704,256]{2,1,0:T(8,128)(2,1)S(1)} %all-to-all-done.8.refs_0_), channel_id=1, source_target_pairs={{0,2},{1,3},{2,0},{3,1},{4,6},{5,7},{6,4},{7,5},{8,10},{9,11},{10,... | collective-permute-start | bytes 8650760 | tf_op jit(solution)/shard_map/cond/branch_0_fun/cond/branch_0_fun/cond/branch_1_fun/ppermute | solution.py:162
  341.1 69.0 %all-to-all-start.7 = ((bf16[8,704,256]{2,1,0:T(8,128)(2,1)}), bf16[8,704,256]{2,1,0:T(8,128)(2,1)}, u32[]{:S(2)}, u32[]{:S(2)}) async-start(bf16[8,704,256]{2,1,0:T(8,128)(2,1)} %coefficients.10), calls=%async_computation.7 | async-start | bytes 5767168 | tf_op jit(solution)/shard_map/cond/branch_0_fun/cond/branch_0_fun/cond/branch_1_fun/all_to_all | solution.py:113
  345.6 5.3 collective-permute-start.10
  345.7 9.5 %collective-permute-start.11 = (bf16[8,704,256]{2,1,0:T(8,128)(2,1)}, bf16[8,704,256]{2,1,0:T(8,128)(2,1)}, u32[]{:S(2)}, u32[]{:S(2)}) collective-permute-start(bf16[8,704,256]{2,1,0:T(8,128)(2,1)} %collective-permute-done.9.refs_1_), channel_id=1, source_target_pairs={{0,1},{1,0},{2,3},{3,2},{4,5},{5,4},{6,7},{7,6},{8,9},{9,8},{10,11... | collective-permute-start | bytes 8650760 | tf_op jit(solution)/shard_map/cond/branch_0_fun/cond/branch_0_fun/cond/branch_1_fun/ppermute | solution.py:162
  350.9 1.6 copy-start.6
  410.1 69.1 %all-to-all-start.9 = ((bf16[8,704,256]{2,1,0:T(8,128)(2,1)}), bf16[8,704,256]{2,1,0:T(8,128)(2,1)S(1)}, u32[]{:S(2)}, u32[]{:S(2)}) async-start(bf16[8,704,256]{2,1,0:T(8,128)(2,1)} %coefficients.11), calls=%async_computation.9 | async-start | bytes 5767168 | tf_op jit(solution)/shard_map/cond/branch_0_fun/cond/branch_0_fun/cond/branch_1_fun/all_to_all | solution.py:113

commit v2 on v1

--- a/solution.py
+++ b/solution.py
@@ -121,18 +121,16 @@
 
 def final_kernel(others, table_ref, value_ref, quad_ref, *refs):
     earlier, out_ref = refs[:others], refs[others]
-    batch, count = table_ref.shape[:2]
+    batch, _, count = table_ref.shape
     for i in range(batch):
         values = value_ref[i].reshape(count, value_ref.shape[-1])
-        summed = lax.dot_general(
-            table_ref[i], values, (((0,), (0,)), ((), ())), preferred_element_type=jnp.float32
-        )
+        summed = jnp.dot(table_ref[i], values, preferred_element_type=jnp.float32)
         parts = [ref[i].astype(jnp.float32) for ref in earlier] + [summed * quad_ref[...]]
         out_ref[i] = jnp.stack(parts, axis=1).astype(jnp.bfloat16)
 
 
 def final_rows(table, values, quad, earlier):
-    slots, count, latitude_count = table.shape
+    slots, latitude_count, count = table.shape
     peers, padded, width = values.shape[1:]
     batch = min(4, slots)
     parts = len(earlier) + 1
@@ -140,7 +138,7 @@
         functools.partial(final_kernel, len(earlier)),
         grid=(-(-slots // batch),),
         in_specs=[
-            pl.BlockSpec((batch, count, latitude_count), lambda i: (i, 0, 0)),
+            pl.BlockSpec((batch, latitude_count, count), lambda i: (i, 0, 0)),
             pl.BlockSpec((batch, peers, padded, width), lambda i: (i, 0, 0, 0)),
             pl.BlockSpec(quad.shape, lambda i: (0, 0)),
         ]
@@ -293,7 +291,7 @@
 
 
 def layer_body(
-    capacity, cotangent, stored_coefficients, weights, order_table, degree_table, mine, owned
+    capacity, cotangent, stored_coefficients, weights, order_table, degree_table, mine
 ):
     slots, latitude_count, batch_size, parts, width = cotangent.shape
     degree_range = stored_coefficients.shape[1]
@@ -319,6 +317,7 @@
     wide_packer = (wide[:, None] == place).astype(jnp.bfloat16)
 
     window = min(-(-slots // 16) * 16 + 16, capacity)
+    owned = lax.dynamic_slice_in_dim(degree_table, lax.axis_index("order") * slots, slots)
     lengths = jnp.sum(
         (
             (order_table.reshape(peers, slots)[None] <= owned[:, None, None])
@@ -351,8 +350,9 @@
     saved = [send_saved(0)]
     table = picked_legendre(mine, degree_table, degree_range, latitude_count)
     table = table.reshape(peers, slots, slots, latitude_count)
-    turned = jnp.pad(table, ((0, 0), (0, spare), (0, 0), (0, 0))).transpose(2, 0, 1, 3)
-    turned = turned.reshape(slots, peers * padded, latitude_count)
+    turned = jnp.pad(table, ((0, 0), (0, spare), (0, 0), (0, 0))).transpose(2, 3, 0, 1)
+    turned = turned.reshape(slots, latitude_count, peers * padded)
+    spread = jnp.broadcast_to(quadrature(latitude_count)[:, None], (latitude_count, width))
     gathered = []
     for r in range(rows):
         blocks, owners = send_adjoint(r)
@@ -376,7 +376,6 @@
             )
             outputs.append((summed * quad[None, :, None]).astype(jnp.bfloat16))
         else:
-            spread = jnp.broadcast_to(quad[:, None], (latitude_count, width))
             outputs = final_rows(turned, returned, spread, outputs)
     mixing_gradient = mixing_gradients(plan, owners, window, gathered, saved, slots)
     return outputs.reshape(cotangent.shape), mixing_gradient
@@ -404,8 +403,7 @@
     peers = lax.axis_size("order")
     position = lax.axis_index("order")
     mine = lax.dynamic_slice_in_dim(order_table, position * slots, slots)
-    owned = lax.dynamic_slice_in_dim(degree_table, position * slots, slots)
-    operands = (cotangent, stored_coefficients, weights, order_table, degree_table, mine, owned)
+    operands = (cotangent, stored_coefficients, weights, order_table, degree_table, mine)
     tiers = capacities(slots, peers, degree_range)
     if len(tiers) == 1:
         return layer_body(tiers[0], *operands)

time: 546 us -> 544 us (level)
  waiting for transfers between devices: 219 us -> 212 us
    all_to_all x6, waiting for transfers between devices: 207 us -> 201 us  [exchange(): lax.all_to_all(value, 'order', split_axis=0, concat_axis=0, tiled=True)]
    reshape x0 -> x1, local copies, waits for them, and re-layouts: none -> 6.36 us  [layer_body(): turned = turned.reshape(slots, latitude_count, peers * padded)]
  transfers between devices with their start and end apart: 12 -> 12, of which waited for: 10 -> 10; matrix products, arithmetic and copies ran while one was open for 13% -> 14% of each run, Pallas kernels for 17% -> 17%
where the time goes in v2:
time: 544 us; the launch traced here: 540 us
  waiting for transfers between devices  212 us (39%)
  Pallas kernels  117 us (22%)
  matrix products  83.4 us (15%)
  local copies, waits for them, and re-layouts  39.1 us (7%)
  loops' own time  39 us (7%)
  starting transfers between devices  33.8 us (6%)
  other arithmetic  10.9 us (2%)
    all_to_all x6, waiting for transfers between devices, exchange(): lax.all_to_all(value, 'order', split_axis=0, concat_axis=0, tiled=True)  201 us
    pallas_call x2, Pallas kernels, coefficients(): pl.pallas_call(kernel, grid_spec=pltpu.PrefetchScalarGridSpec(num_scalar_...  59.8 us
    dot_general x4, matrix products, pack(): jnp.einsum('tpks,tksc->tpc', packer, value, preferred_element_type=jnp.fl...  40.5 us
    another operation x3, loops' own time, choose(): lax.cond(tier == 0, first, lambda *rest: choose(tier - 1, tiers[1:], rest...  39 us
    pallas_call x1, Pallas kernels, mixing_gradients(): pl.pallas_call(functools.partial(mixing_kernel, peers, window, blocks, ro...  33.1 us
    all_to_all x6, starting transfers between devices, exchange(): lax.all_to_all(value, 'order', split_axis=0, concat_axis=0, tiled=True)  29.5 us
    dot_general x4, matrix products, project(): jnp.einsum('tksj,sjc->tksc', matrix, source, preferred_element_type=jnp.f...  23.5 us
    pallas_call x1, Pallas kernels, final_rows(): pl.pallas_call(functools.partial(final_kernel, len(earlier)), grid=(-(-sl...  16.7 us
  transfers between devices with their start and end apart: 12, of which 10 were waited for; matrix products, arithmetic and copies ran while one was open for 14% of the time, Pallas kernels for 17%

profile of v2, /device:TPU:0, one launch (start us, length us, event | category | flops | bytes accessed | tf_op | source)
XLA Modules:
  0.0 539.7 jit_solution(2570965651464303281)
XLA Ops:
  0.6 0.8 ge.137
  1.4 0.8 ge.139
  2.2 0.5 convert_reduce_fusion.4
  2.7 0.6 reduce_max.9
  5.3 0.8 dynamic_slice.15
  6.0 532.4 %conditional.3 = ((bf16[31,240,1,2,256]{4,3,1,0,2:T(2,128)(2,1)}, bf16[31,256,1024]{2,1,0:T(8,128)(2,1)})) conditional(s32[]{:T(128)} %convert_element_type.554, (s32[]{:T(128)}, s32[248]{0:T(256)}, s32[31]{0:T(128)S(1)}, s32[248]{0:T(256)}, s32[4]{0:T(128)}, /*index=5*/bf16[31,240,1,2,256]{4,3,2,1,0:T(2,128)(2,1)}, ...), branch_computations={%region_2.19_spmd, %region_19.24_spmd} | conditional | flops 53937319936 | bytes 551175040 | solution.py:397
  6.1 7.4 %copy.271 = bf16[31,240,1,2,256]{4,1,0,3,2:T(8,128)(2,1)} copy(bf16[31,240,1,2,256]{4,3,2,1,0:T(2,128)(2,1)} %get-tuple-element.211) | data formatting | bytes 15237120 | tf_op jit(solution)/shard_map
  13.5 4.2 copy.272
  17.7 504.6 %conditional.1 = ((bf16[31,240,1,2,256]{4,3,1,0,2:T(2,128)(2,1)}, bf16[31,256,1024]{2,1,0:T(8,128)(2,1)})) conditional(s32[]{:T(128)} %convert_element_type.513, (s32[]{:T(128)}, s32[248]{0:T(256)S(1)}, s32[31]{0:T(128)S(1)}, s32[248]{0:T(256)}, s32[4]{0:T(128)}, /*index=5*/bf16[31,240,1,2,256]{4,1,0,3,2:T(8,128)(2,1)}, ...), branch_computations={%region_3.13_spmd, %region_14.18_spmd} | conditional | flops 53937319936 | bytes 497840896 | solution.py:397
  17.7 489.3 %conditional = (bf16[31,240,1,2,256]{4,3,1,0,2:T(2,128)(2,1)}, bf16[31,256,1024]{2,1,0:T(8,128)(2,1)}) conditional(s32[]{:T(128)} %convert_element_type.481, (s32[248]{0:T(256)S(1)}, s32[31]{0:T(128)S(1)}, s32[248]{0:T(256)}, s32[4]{0:T(128)}, bf16[31,240,1,2,256]{4,1,0,3,2:T(8,128)(2,1)}, /*index=5*/bf16[31,256,1024]{2,1,0:T(8,128)(2,1)}, ...), branch_computations={%region_4.7_spmd, %region_9.12_spmd} | conditional | flops 53937319936 | bytes 497840768 | solution.py:397
  25.0 0.2 select_reduce_fusion.3
  25.6 0.6 broadcast_minimum_fusion.1.where_ref
  26.8 0.3 fusion.137
  27.1 0.2 eq.182
  27.3 0.7 exponential_multiply_fusion.1.start_ref
  28.0 2.5 broadcast_in_dim.115.upper_ref
  30.5 2.5 broadcast_in_dim.116.lower_ref
  33.0 0.7 broadcast_in_dim.117.order_ref
  33.7 0.6 broadcast_in_dim.118.cosine_ref
  34.3 7.5 %legendre.5 = bf16[248,31,240]{2,1,0:T(8,128)(2,1)} custom-call(s32[240]{0:T(256)} %broadcast_minimum_fusion.1.where_ref, f32[240,31,128]{2,1,0:T(8,128)} %broadcast_in_dim.115.upper_ref, f32[240,31,128]{2,1,0:T(8,128)} %broadcast_in_dim.116.lower_ref, s32[31,128]{1,0:T(8,128)} %broadcast_in_dim.117.order_ref, f32[31,240]{1,0:T(8,128)} %broadcast_in_dim.118.cosine_ref, ...), custom_call_target="tpu_custom_call" | custom-call | flops 10713600 | bytes 25165824 | tf_op jit(solution)/shard_map/cond/branch_0_fun/cond/branch_0_fun/cond/branch_1_fun/legendre/pallas_call | solution.py:86
  41.8 7.9 %convert_bitcast_fusion.7 = bf16[8,31,31,256]{3,1,0,2:T(8,128)(2,1)S(1)} fusion(bf16[31,240,2,256]{3,1,0,2:T(8,128)(2,1)} %bitcast.428, bf16[8,31,31,240]{3,2,1,0:T(8,128)(2,1)} %bitcast.410), kind=kOutput, calls=%fused_computation.145 | convolution fusion | flops 946669568 | bytes 11808768 | tf_op jit(solution)/shard_map/cond/branch_0_fun/cond/branch_0_fun/cond/branch_1_fun/tksj,sjc->tksc/dot_general | solution.py:339
  49.7 10.2 %bitcast_convert_fusion.6 = bf16[8,704,256]{2,1,0:T(8,128)(2,1)} fusion(bf16[8,31,31,256]{3,1,0,2:T(8,128)(2,1)S(1)} %convert_bitcast_fusion.7, s32[8,31,31]{2,1,0:T(8,128)S(1)} %eq.182), kind=kOutput, calls=%fused_computation.135 | convolution fusion | flops 2777978368 | bytes 6850592 | tf_op jit(solution)/shard_map/cond/branch_0_fun/cond/branch_0_fun/cond/branch_1_fun/tpks,tksc->tpc/dot_general | solution.py:117
  59.8 7.7 %all-to-all-start.8 = ((bf16[8,704,256]{2,1,0:T(8,128)(2,1)}), bf16[8,704,256]{2,1,0:T(8,128)(2,1)S(1)}, u32[]{:S(2)}, u32[]{:S(2)}) async-start(bf16[8,704,256]{2,1,0:T(8,128)(2,1)} %bitcast_convert_fusion.6), calls=%async_computation.8 | async-start | bytes 5767168 | tf_op jit(solution)/shard_map/cond/branch_0_fun/cond/branch_0_fun/cond/branch_1_fun/all_to_all | solution.py:113
  67.6 7.9 %convert_bitcast_fusion.9 = bf16[8,31,31,256]{3,1,0,2:T(8,128)(2,1)S(1)} fusion(bf16[31,240,2,256]{3,1,0,2:T(8,128)(2,1)} %bitcast.429, bf16[8,31,31,240]{3,2,1,0:T(8,128)(2,1)} %bitcast.411), kind=kOutput, calls=%fused_computation.147 | convolution fusion | flops 946669568 | bytes 11808768 | tf_op jit(solution)/shard_map/cond/branch_0_fun/cond/branch_0_fun/cond/branch_1_fun/tksj,sjc->tksc/dot_general | solution.py:339
  75.5 10.2 %bitcast_convert_fusion.7 = bf16[8,704,256]{2,1,0:T(8,128)(2,1)} fusion(bf16[8,31,31,256]{3,1,0,2:T(8,128)(2,1)S(1)} %convert_bitcast_fusion.9, s32[8,31,31]{2,1,0:T(8,128)S(1)} %eq.182), kind=kOutput, calls=%fused_computation.136 | convolution fusion | flops 2777978368 | bytes 6850592 | tf_op jit(solution)/shard_map/cond/branch_0_fun/cond/branch_0_fun/cond/branch_1_fun/tpks,tksc->tpc/dot_general | solution.py:117
  85.6 47.0 %all-to-all-done.8.refs_0_ = bf16[8,704,256]{2,1,0:T(8,128)(2,1)S(1)} async-done(((bf16[8,704,256]{2,1,0:T(8,128)(2,1)}), bf16[8,704,256]{2,1,0:T(8,128)(2,1)S(1)}, u32[]{:S(2)}, u32[]{:S(2)}) %all-to-all-start.8) | async-done | bytes 2883616 | tf_op jit(solution)/shard_map/cond/branch_0_fun/cond/branch_0_fun/cond/branch_1_fun/all_to_all | solution.py:113
  132.6 4.5 all-to-all-start.6
  137.5 3.8 convert_bitcast_fusion.6
  141.3 10.1 %bitcast_convert_fusion.5 = bf16[8,704,256]{2,1,0:T(8,128)(2,1)} fusion(bf16[8,31,31,256]{3,1,0,2:T(8,128)(2,1)S(1)} %convert_bitcast_fusion.6, s32[8,31,31]{2,1,0:T(8,128)S(1)} %eq.182), kind=kOutput, calls=%fused_computation.134 | convolution fusion | flops 2777978368 | bytes 6850592 | tf_op jit(solution)/shard_map/cond/branch_0_fun/cond/branch_0_fun/cond/branch_1_fun/tpks,tksc->tpc/dot_general | solution.py:117
  151.4 50.2 %all-to-all-done.6.refs_0_.refs_4_ = bf16[8,704,256]{2,1,0:T(8,128)(2,1)} async-done(((bf16[8,704,256]{2,1,0:T(8,128)(2,1)}), bf16[8,704,256]{2,1,0:T(8,128)(2,1)}, u32[]{:S(2)}, u32[]{:S(2)}) %all-to-all-start.6) | async-done | bytes 2883616 | tf_op jit(solution)/shard_map/cond/branch_0_fun/cond/branch_0_fun/cond/branch_1_fun/all_to_all | solution.py:113
  201.6 4.6 all-to-all-start.10
  206.3 3.9 convert_bitcast_fusion.5
  210.1 1.6 collective-permute-start.6
  211.7 10.1 %bitcast_convert_fusion.4 = bf16[8,704,256]{2,1,0:T(8,128)(2,1)} fusion(bf16[8,31,31,256]{3,1,0,2:T(8,128)(2,1)S(1)} %convert_bitcast_fusion.5, s32[8,31,31]{2,1,0:T(8,128)S(1)} %eq.182), kind=kOutput, calls=%fused_computation.133 | convolution fusion | flops 2777978368 | bytes 6850592 | tf_op jit(solution)/shard_map/cond/branch_0_fun/cond/branch_0_fun/cond/branch_1_fun/tpks,tksc->tpc/dot_general | solution.py:117
  221.8 49.0 %all-to-all-done.10.refs_8_ = bf16[8,704,256]{2,1,0:T(8,128)(2,1)} async-done(((bf16[8,704,256]{2,1,0:T(8,128)(2,1)}), bf16[8,704,256]{2,1,0:T(8,128)(2,1)}, u32[]{:S(2)}, u32[]{:S(2)}) %all-to-all-start.10) | async-done | bytes 2883616 | tf_op jit(solution)/shard_map/cond/branch_0_fun/cond/branch_0_fun/cond/branch_1_fun/all_to_all | solution.py:113
  270.8 4.5 all-to-all-start.11
  275.4 0.5 collective-permute-start.8
  276.0 0.7 convert_reduce_fusion.1
  276.7 1.6 collective-permute-start.9
  278.4 0.6 multiply_reduce_fusion.1
  279.3 0.8 reshape.1119.plan_ref
  280.1 0.6 broadcast_xor_fusion.1.owner_ref
  280.6 0.3 collective-permute-done.7.refs_2_.refs_6_
  281.0 4.1 collective-permute-done.8.refs_3_.refs_7_
  285.1 29.9 %coefficients.10 = bf16[8,704,256]{2,1,0:T(8,128)(2,1)} custom-call(s32[744]{0:T(1024)} %reshape.1119.plan_ref, s32[4]{0:T(128)} %broadcast_xor_fusion.1.owner_ref, bf16[8,704,256]{2,1,0:T(8,128)(2,1)} %all-to-all-done.6.refs_0_.refs_4_, bf16[8,704,256]{2,1,0:T(8,128)(2,1)} %collective-permute-done.6.refs_1_.refs_5_, ...), custom_call_target="tpu_custom_call" | custom-call | flops 6241124352 | bytes 30670848 | tf_op jit(solution)/shard_map/cond/branch_0_fun/cond/branch_0_fun/cond/branch_1_fun/coefficients/pallas_call | solution.py:246
  315.0 24.9 %all-to-all-done.11.refs_9_ = bf16[8,704,256]{2,1,0:T(8,128)(2,1)} async-done(((bf16[8,704,256]{2,1,0:T(8,128)(2,1)}), bf16[8,704,256]{2,1,0:T(8,128)(2,1)}, u32[]{:S(2)}, u32[]{:S(2)}) %all-to-all-start.11) | async-done | bytes 2883616 | tf_op jit(solution)/shard_map/cond/branch_0_fun/cond/branch_0_fun/cond/branch_1_fun/all_to_all | solution.py:113
  339.8 4.4 all-to-all-start.7
  344.4 0.5 collective-permute-start.11
  344.9 4.8 collective-permute-done.10.refs_2_
  349.7 1.6 copy-done.6
  351.2 2.7 collective-permute-done.11.refs_3_
  353.9 29.9 %coefficients.11 = bf16[8,704,256]{2,1,0:T(8,128)(2,1)} custom-call(s32[744]{0:T(1024)} %reshape.1119.plan_ref, s32[4]{0:T(128)} %broadcast_xor_fusion.1.owner_ref, bf16[8,704,256]{2,1,0:T(8,128)(2,1)} %copy-done.2, bf16[8,704,256]{2,1,0:T(8,128)(2,1)} %collective-permute-done.9.refs_1_, bf16[8,704,256]{2,1,0:T(8,128)(2,1)} %copy-done.6, ...), custom_call_target="tpu_custom_call" | custom-call | flops 6241124352 | bytes 30670848 | tf_op jit(solution)/shard_map/cond/branch_0_fun/cond/branch_0_fun/cond/branch_1_fun/coefficients/pallas_call | solution.py:246
  383.8 25.0 %all-to-all-done.7 = bf16[8,704,256]{2,1,0:T(8,128)(2,1)} async-done(((bf16[8,704,256]{2,1,0:T(8,128)(2,1)}), bf16[8,704,256]{2,1,0:T(8,128)(2,1)}, u32[]{:S(2)}, u32[]{:S(2)}) %all-to-all-start.7) | async-done | bytes 2883616 | tf_op jit(solution)/shard_map/cond/branch_0_fun/cond/branch_0_fun/cond/branch_1_fun/all_to_all | solution.py:113
  408.9 3.9 all-to-all-start.9
  412.9 4.5 copy.216
  417.3 3.2 pad.20
  420.5 6.4 %copy.229.table_ref = bf16[31,240,256]{2,1,0:T(8,128)(2,1)} copy(bf16[31,240,256]{1,2,0:T(8,128)(2,1)} %bitcast.423) | data formatting | bytes 7618560 | tf_op jit(solution)/shard_map/cond/branch_0_fun/cond/branch_0_fun/cond/branch_1_fun/reshape | solution.py:354
  426.9 5.6 %iota_compare_fusion.24 = pred[8,704,31,31]{1,3,2,0:T(8,128)(4,1)} fusion(s32[8,31,31]{2,1,0:T(8,128)S(1)} %eq.182), kind=kLoop, calls=%fused_computation.114 | loop fusion | flops 5412352 | bytes 5443104 | tf_op jit(solution)/shard_map/cond/branch_0_fun/cond/branch_0_fun/cond/branch_1_fun/eq | solution.py:312
  432.5 33.1 %mixing.5 = bf16[31,256,1024]{2,1,0:T(8,128)(2,1)} custom-call(s32[744]{0:T(1024)} %reshape.1119.plan_ref, s32[4]{0:T(128)} %broadcast_xor_fusion.1.owner_ref, bf16[8,704,256]{2,1,0:T(8,128)(2,1)} %copy-done.2, bf16[8,704,256]{2,1,0:T(8,128)(2,1)} %collective-permute-done.9.refs_1_, bf16[8,704,256]{2,1,0:T(8,128)(2,1)} %copy-done.6, ...), custom_call_target="tpu_custom_call" | custom-call | flops 12482248704 | bytes 45088768 | tf_op jit(solution)/shard_map/cond/branch_0_fun/cond/branch_0_fun/cond/branch_1_fun/mixing/pallas_call | solution.py:270
  465.7 7.8 %convert_bitcast_fusion.8.value_ref = bf16[31,8,32,256]{3,2,1,0:T(8,128)(2,1)} fusion(bf16[8,704,256]{2,1,0:T(8,128)(2,1)} %all-to-all-done.7, s32[8,32,31]{1,2,0:T(8,128)S(1)} %pad.21.clone), kind=kOutput, calls=%fused_computation.146 | convolution fusion | flops 2868133888 | bytes 6978560 | tf_op jit(solution)/shard_map/cond/branch_0_fun/cond/branch_0_fun/cond/branch_1_fun/tpks,tpc->stkc/dot_general | solution.py:367
  473.4 4.5 all-to-all-done.9
  477.9 11.3 %fusion.102.refs_0_ = bf16[31,240,256]{2,1,0:T(8,128)(2,1)} fusion(f32[240]{0:T(256)S(1)} %fusion.155, bf16[8,31,31,240]{3,2,1,0:T(8,128)(2,1)} %bitcast.413, pred[8,704,31,31]{1,3,2,0:T(8,128)(4,1)} %iota_compare_fusion.24, bf16[8,704,256]{2,1,0:T(8,128)(2,1)S(1)} %all-to-all-done.9), kind=kOutput, calls=%fused_computation.132 | convolution fusion | flops 3721603072 | bytes 15796416 | tf_op jit(solution)/shard_map/cond/branch_0_fun/cond/branch_0_fun/cond/branch_1_fun/tksj,tksc->sjc/dot_general | solution.py:374
  489.3 0.8 broadcast_in_dim.120.quad_ref
  490.1 16.7 %final.5 = bf16[31,240,2,256]{3,2,1,0:T(2,128)(2,1)} custom-call(bf16[31,240,256]{2,1,0:T(8,128)(2,1)} %copy.229.table_ref, bf16[31,8,32,256]{3,2,1,0:T(8,128)(2,1)} %convert_bitcast_fusion.8.value_ref, f32[240,256]{1,0:T(8,128)} %broadcast_in_dim.120.quad_ref, bf16[31,240,256]{2,1,0:T(8,128)(2,1)} %fusion.102.refs_0_), custom_call_target="tpu_custom_call" | custom-call | flops 975175680 | bytes 23109632 | tf_op jit(solution)/shard_map/cond/branch_0_fun/cond/branch_0_fun/cond/branch_1_fun/final/pallas_call | solution.py:137
  (62 shorter events, 2.6 us)
Async XLA Ops:
  6.0 7.4 %slice-start = ((s8[7618560]{0:T(1024)(128)(4,1)}), s8[4194304]{0:T(1024)(128)(4,1)S(1)}, s32[]{:S(2)}) async-start(s8[7618560]{0:T(1024)(128)(4,1)} %bitcast.404), calls=%async_computation.24 | async-start | bytes 8388608 | tf_op jit(solution)/shard_map/cond
  6.0 7.4 %slice-start.1 = ((s8[7618560]{0:T(1024)(128)(4,1)}), s8[3424256]{0:T(1024)(128)(4,1)S(1)}, s32[]{:S(2)}) async-start(s8[7618560]{0:T(1024)(128)(4,1)} %bitcast.404), calls=%async_computation.25 | async-start | bytes 6848512 | tf_op jit(solution)/shard_map/cond
  13.5 4.2 copy-start.14
  24.7 0.6 copy-start.17
  24.7 8.3 %copy-start.8 = (s32[31]{0:T(128)}, s32[31]{0:T(128)S(1)}, u32[]{:S(2)}) copy-start(s32[31]{0:T(128)S(1)} %get-tuple-element.102) | copy-start | bytes 376 | tf_op jit(solution)/shard_map/cond/branch_0_fun/cond/branch_0_fun/cond
  59.8 72.8 %all-to-all-start.8 = ((bf16[8,704,256]{2,1,0:T(8,128)(2,1)}), bf16[8,704,256]{2,1,0:T(8,128)(2,1)S(1)}, u32[]{:S(2)}, u32[]{:S(2)}) async-start(bf16[8,704,256]{2,1,0:T(8,128)(2,1)} %bitcast_convert_fusion.6), calls=%async_computation.8 | async-start | bytes 5767168 | tf_op jit(solution)/shard_map/cond/branch_0_fun/cond/branch_0_fun/cond/branch_1_fun/all_to_all | solution.py:113
  85.6 51.5 %copy-start.9 = (s32[31]{0:T(128)S(1)}, s32[31]{0:T(128)}, u32[]{:S(2)}) copy-start(s32[31]{0:T(128)} %copy-done.8) | copy-start | bytes 376 | tf_op jit(solution)/shard_map/cond/branch_0_fun/cond/branch_0_fun/cond
  132.6 211.7 %copy-start.2 = (bf16[8,704,256]{2,1,0:T(8,128)(2,1)}, bf16[8,704,256]{2,1,0:T(8,128)(2,1)S(1)}, u32[]{:S(2)}) copy-start(bf16[8,704,256]{2,1,0:T(8,128)(2,1)S(1)} %all-to-all-done.8.refs_0_) | copy-start | bytes 8650756 | tf_op jit(solution)/shard_map/cond/branch_0_fun/cond/branch_0_fun/cond
  132.6 69.0 %all-to-all-start.6 = ((bf16[8,704,256]{2,1,0:T(8,128)(2,1)}), bf16[8,704,256]{2,1,0:T(8,128)(2,1)}, u32[]{:S(2)}, u32[]{:S(2)}) async-start(bf16[8,704,256]{2,1,0:T(8,128)(2,1)} %bitcast_convert_fusion.7), calls=%async_computation.6 | async-start | bytes 5767168 | tf_op jit(solution)/shard_map/cond/branch_0_fun/cond/branch_0_fun/cond/branch_1_fun/all_to_all | solution.py:113
  201.6 69.2 %all-to-all-start.10 = ((bf16[8,704,256]{2,1,0:T(8,128)(2,1)}), bf16[8,704,256]{2,1,0:T(8,128)(2,1)}, u32[]{:S(2)}, u32[]{:S(2)}) async-start(bf16[8,704,256]{2,1,0:T(8,128)(2,1)} %bitcast_convert_fusion.5), calls=%async_computation.10 | async-start | bytes 5767168 | tf_op jit(solution)/shard_map/cond/branch_0_fun/cond/branch_0_fun/cond/branch_1_fun/all_to_all | solution.py:113
  210.1 65.2 %collective-permute-start.6 = (bf16[8,704,256]{2,1,0:T(8,128)(2,1)}, bf16[8,704,256]{2,1,0:T(8,128)(2,1)}, u32[]{:S(2)}, u32[]{:S(2)}) collective-permute-start(bf16[8,704,256]{2,1,0:T(8,128)(2,1)} %all-to-all-done.6.refs_0_.refs_4_), channel_id=1, source_target_pairs={{0,2},{1,3},{2,0},{3,1},{4,6},{5,7},{6,4},{7,5},{8,10},{9,11},{10,... | collective-permute-start | bytes 8650760 | tf_op jit(solution)/shard_map/cond/branch_0_fun/cond/branch_0_fun/cond/branch_1_fun/ppermute | solution.py:160
  221.8 54.1 %copy-start.23 = (s32[248]{0:T(256)S(1)}, s32[248]{0:T(256)}, u32[]{:S(2)}) copy-start(s32[248]{0:T(256)} %get-tuple-element.103) | copy-start | bytes 2980 | tf_op jit(solution)/shard_map/cond/branch_0_fun/cond/branch_0_fun/cond
  221.8 54.1 %copy-start.18 = (s32[248]{0:T(256)S(1)}, s32[248]{0:T(256)}, u32[]{:S(2)}) copy-start(s32[248]{0:T(256)} %copy-done.17) | copy-start | bytes 2980 | tf_op jit(solution)/shard_map/cond/branch_0_fun/cond/branch_0_fun/cond
  221.8 58.3 %copy-start.27 = (s32[4]{0:T(128)S(1)}, s32[4]{0:T(128)}, u32[]{:S(2)}) copy-start(s32[4]{0:T(128)} %get-tuple-element.104) | copy-start | bytes 52 | tf_op jit(solution)/shard_map/cond/branch_0_fun/cond/branch_0_fun/cond
  270.8 69.0 %all-to-all-start.11 = ((bf16[8,704,256]{2,1,0:T(8,128)(2,1)}), bf16[8,704,256]{2,1,0:T(8,128)(2,1)}, u32[]{:S(2)}, u32[]{:S(2)}) async-start(bf16[8,704,256]{2,1,0:T(8,128)(2,1)} %bitcast_convert_fusion.4), calls=%async_computation.11 | async-start | bytes 5767168 | tf_op jit(solution)/shard_map/cond/branch_0_fun/cond/branch_0_fun/cond/branch_1_fun/all_to_all | solution.py:113
  275.3 5.7 %collective-permute-start.7 = (bf16[8,704,256]{2,1,0:T(8,128)(2,1)}, bf16[8,704,256]{2,1,0:T(8,128)(2,1)}, u32[]{:S(2)}, u32[]{:S(2)}) collective-permute-start(bf16[8,704,256]{2,1,0:T(8,128)(2,1)} %all-to-all-done.6.refs_0_.refs_4_), channel_id=1, source_target_pairs={{0,1},{1,0},{2,3},{3,2},{4,5},{5,4},{6,7},{7,6},{8,9},{9,8},{10,11... | collective-permute-start | bytes 8650760 | tf_op jit(solution)/shard_map/cond/branch_0_fun/cond/branch_0_fun/cond/branch_1_fun/ppermute | solution.py:160
  275.4 9.7 %collective-permute-start.8 = (bf16[8,704,256]{2,1,0:T(8,128)(2,1)}, bf16[8,704,256]{2,1,0:T(8,128)(2,1)}, u32[]{:S(2)}, u32[]{:S(2)}) collective-permute-start(bf16[8,704,256]{2,1,0:T(8,128)(2,1)} %collective-permute-done.6.refs_1_.refs_5_), channel_id=1, source_target_pairs={{0,1},{1,0},{2,3},{3,2},{4,5},{5,4},{6,7},{7,6},{8,9},{9,8},{10,11... | collective-permute-start | bytes 8650760 | tf_op jit(solution)/shard_map/cond/branch_0_fun/cond/branch_0_fun/cond/branch_1_fun/ppermute | solution.py:160
  276.7 67.7 %collective-permute-start.9 = (bf16[8,704,256]{2,1,0:T(8,128)(2,1)S(1)}, bf16[8,704,256]{2,1,0:T(8,128)(2,1)}, u32[]{:S(2)}, u32[]{:S(2)}) collective-permute-start(bf16[8,704,256]{2,1,0:T(8,128)(2,1)S(1)} %all-to-all-done.8.refs_0_), channel_id=1, source_target_pairs={{0,2},{1,3},{2,0},{3,1},{4,6},{5,7},{6,4},{7,5},{8,10},{9,11},{10,... | collective-permute-start | bytes 8650760 | tf_op jit(solution)/shard_map/cond/branch_0_fun/cond/branch_0_fun/cond/branch_1_fun/ppermute | solution.py:160
  339.8 69.0 %all-to-all-start.7 = ((bf16[8,704,256]{2,1,0:T(8,128)(2,1)}), bf16[8,704,256]{2,1,0:T(8,128)(2,1)}, u32[]{:S(2)}, u32[]{:S(2)}) async-start(bf16[8,704,256]{2,1,0:T(8,128)(2,1)} %coefficients.10), calls=%async_computation.7 | async-start | bytes 5767168 | tf_op jit(solution)/shard_map/cond/branch_0_fun/cond/branch_0_fun/cond/branch_1_fun/all_to_all | solution.py:113
  344.3 5.3 collective-permute-start.10
  344.4 9.5 %collective-permute-start.11 = (bf16[8,704,256]{2,1,0:T(8,128)(2,1)}, bf16[8,704,256]{2,1,0:T(8,128)(2,1)}, u32[]{:S(2)}, u32[]{:S(2)}) collective-permute-start(bf16[8,704,256]{2,1,0:T(8,128)(2,1)} %collective-permute-done.9.refs_1_), channel_id=1, source_target_pairs={{0,1},{1,0},{2,3},{3,2},{4,5},{5,4},{6,7},{7,6},{8,9},{9,8},{10,11... | collective-permute-start | bytes 8650760 | tf_op jit(solution)/shard_map/cond/branch_0_fun/cond/branch_0_fun/cond/branch_1_fun/ppermute | solution.py:160
  349.7 1.6 copy-start.6
  408.9 69.1 %all-to-all-start.9 = ((bf16[8,704,256]{2,1,0:T(8,128)(2,1)}), bf16[8,704,256]{2,1,0:T(8,128)(2,1)S(1)}, u32[]{:S(2)}, u32[]{:S(2)}) async-start(bf16[8,704,256]{2,1,0:T(8,128)(2,1)} %coefficients.11), calls=%async_computation.9 | async-start | bytes 5767168 | tf_op jit(solution)/shard_map/cond/branch_0_fun/cond/branch_0_fun/cond/branch_1_fun/all_to_all | solution.py:113

commit v3 on v2

--- a/solution.py
+++ b/solution.py
@@ -125,8 +125,9 @@
     for i in range(batch):
         values = value_ref[i].reshape(count, value_ref.shape[-1])
         summed = jnp.dot(table_ref[i], values, preferred_element_type=jnp.float32)
-        parts = [ref[i].astype(jnp.float32) for ref in earlier] + [summed * quad_ref[...]]
-        out_ref[i] = jnp.stack(parts, axis=1).astype(jnp.bfloat16)
+        for r, ref in enumerate(earlier):
+            out_ref[i, :, r, :] = ref[i]
+        out_ref[i, :, others, :] = (summed * quad_ref[...]).astype(jnp.bfloat16)
 
 
 def final_rows(table, values, quad, earlier):

time: 544 us -> 542 us (level)
  no operation moved by 1% of the time
where the time goes in v3:
time: 542 us; the launch traced here: 537 us
  waiting for transfers between devices  212 us (39%)
  Pallas kernels  114 us (21%)
  matrix products  83.4 us (15%)
  loops' own time  39.2 us (7%)
  local copies, waits for them, and re-layouts  39.1 us (7%)
  starting transfers between devices  33.8 us (6%)
  other arithmetic  10.9 us (2%)
    all_to_all x6, waiting for transfers between devices, exchange(): lax.all_to_all(value, 'order', split_axis=0, concat_axis=0, tiled=True)  201 us
    pallas_call x2, Pallas kernels, coefficients(): pl.pallas_call(kernel, grid_spec=pltpu.PrefetchScalarGridSpec(num_scalar_...  59.8 us
    dot_general x4, matrix products, pack(): jnp.einsum('tpks,tksc->tpc', packer, value, preferred_element_type=jnp.fl...  40.5 us
    another operation x3, loops' own time, choose(): lax.cond(tier == 0, first, lambda *rest: choose(tier - 1, tiers[1:], rest...  39.2 us
    pallas_call x1, Pallas kernels, mixing_gradients(): pl.pallas_call(functools.partial(mixing_kernel, peers, window, blocks, ro...  33.1 us
    all_to_all x6, starting transfers between devices, exchange(): lax.all_to_all(value, 'order', split_axis=0, concat_axis=0, tiled=True)  29.5 us
    dot_general x4, matrix products, project(): jnp.einsum('tksj,sjc->tksc', matrix, source, preferred_element_type=jnp.f...  23.5 us
    pallas_call x1, Pallas kernels, final_rows(): pl.pallas_call(functools.partial(final_kernel, len(earlier)), grid=(-(-sl...  13.7 us
  transfers between devices with their start and end apart: 12, of which 10 were waited for; matrix products, arithmetic and copies ran while one was open for 14% of the time, Pallas kernels for 17%

profile of v3, /device:TPU:0, one launch (start us, length us, event | category | flops | bytes accessed | tf_op | source)
XLA Modules:
  0.0 536.8 jit_solution(4801594546423346677)
XLA Ops:
  0.6 0.8 ge.137
  1.4 0.8 ge.139
  2.2 0.5 convert_reduce_fusion.4
  2.7 0.6 reduce_max.9
  5.3 0.8 dynamic_slice.15
  6.0 529.7 %conditional.3 = ((bf16[31,240,1,2,256]{4,3,1,0,2:T(2,128)(2,1)}, bf16[31,256,1024]{2,1,0:T(8,128)(2,1)})) conditional(s32[]{:T(128)} %convert_element_type.554, (s32[]{:T(128)}, s32[248]{0:T(256)}, s32[31]{0:T(128)S(1)}, s32[248]{0:T(256)}, s32[4]{0:T(128)}, /*index=5*/bf16[31,240,1,2,256]{4,3,2,1,0:T(2,128)(2,1)}, ...), branch_computations={%region_2.19_spmd, %region_19.24_spmd} | conditional | flops 53937319936 | bytes 551175040 | solution.py:398
  6.1 7.4 %copy.271 = bf16[31,240,1,2,256]{4,1,0,3,2:T(8,128)(2,1)} copy(bf16[31,240,1,2,256]{4,3,2,1,0:T(2,128)(2,1)} %get-tuple-element.211) | data formatting | bytes 15237120 | tf_op jit(solution)/shard_map
  13.5 4.2 copy.272
  17.7 502.0 %conditional.1 = ((bf16[31,240,1,2,256]{4,3,1,0,2:T(2,128)(2,1)}, bf16[31,256,1024]{2,1,0:T(8,128)(2,1)})) conditional(s32[]{:T(128)} %convert_element_type.513, (s32[]{:T(128)}, s32[248]{0:T(256)S(1)}, s32[31]{0:T(128)S(1)}, s32[248]{0:T(256)}, s32[4]{0:T(128)}, /*index=5*/bf16[31,240,1,2,256]{4,1,0,3,2:T(8,128)(2,1)}, ...), branch_computations={%region_3.13_spmd, %region_14.18_spmd} | conditional | flops 53937319936 | bytes 497840896 | solution.py:398
  17.7 486.6 %conditional = (bf16[31,240,1,2,256]{4,3,1,0,2:T(2,128)(2,1)}, bf16[31,256,1024]{2,1,0:T(8,128)(2,1)}) conditional(s32[]{:T(128)} %convert_element_type.481, (s32[248]{0:T(256)S(1)}, s32[31]{0:T(128)S(1)}, s32[248]{0:T(256)}, s32[4]{0:T(128)}, bf16[31,240,1,2,256]{4,1,0,3,2:T(8,128)(2,1)}, /*index=5*/bf16[31,256,1024]{2,1,0:T(8,128)(2,1)}, ...), branch_computations={%region_4.7_spmd, %region_9.12_spmd} | conditional | flops 53937319936 | bytes 497840768 | solution.py:398
  25.4 0.2 select_reduce_fusion.3
  25.9 0.6 broadcast_minimum_fusion.1.where_ref
  27.1 0.3 fusion.137
  27.4 0.2 eq.182
  27.6 0.7 exponential_multiply_fusion.1.start_ref
  28.3 2.5 broadcast_in_dim.115.upper_ref
  30.8 2.5 broadcast_in_dim.116.lower_ref
  33.3 0.7 broadcast_in_dim.117.order_ref
  34.0 0.6 broadcast_in_dim.118.cosine_ref
  34.6 7.5 %legendre.5 = bf16[248,31,240]{2,1,0:T(8,128)(2,1)} custom-call(s32[240]{0:T(256)} %broadcast_minimum_fusion.1.where_ref, f32[240,31,128]{2,1,0:T(8,128)} %broadcast_in_dim.115.upper_ref, f32[240,31,128]{2,1,0:T(8,128)} %broadcast_in_dim.116.lower_ref, s32[31,128]{1,0:T(8,128)} %broadcast_in_dim.117.order_ref, f32[31,240]{1,0:T(8,128)} %broadcast_in_dim.118.cosine_ref, ...), custom_call_target="tpu_custom_call" | custom-call | flops 10713600 | bytes 25165824 | tf_op jit(solution)/shard_map/cond/branch_0_fun/cond/branch_0_fun/cond/branch_1_fun/legendre/pallas_call | solution.py:86
  42.1 7.9 %convert_bitcast_fusion.7 = bf16[8,31,31,256]{3,1,0,2:T(8,128)(2,1)S(1)} fusion(bf16[31,240,2,256]{3,1,0,2:T(8,128)(2,1)} %bitcast.428, bf16[8,31,31,240]{3,2,1,0:T(8,128)(2,1)} %bitcast.410), kind=kOutput, calls=%fused_computation.145 | convolution fusion | flops 946669568 | bytes 11808768 | tf_op jit(solution)/shard_map/cond/branch_0_fun/cond/branch_0_fun/cond/branch_1_fun/tksj,sjc->tksc/dot_general | solution.py:340
  50.0 10.2 %bitcast_convert_fusion.6 = bf16[8,704,256]{2,1,0:T(8,128)(2,1)} fusion(bf16[8,31,31,256]{3,1,0,2:T(8,128)(2,1)S(1)} %convert_bitcast_fusion.7, s32[8,31,31]{2,1,0:T(8,128)S(1)} %eq.182), kind=kOutput, calls=%fused_computation.135 | convolution fusion | flops 2777978368 | bytes 6850592 | tf_op jit(solution)/shard_map/cond/branch_0_fun/cond/branch_0_fun/cond/branch_1_fun/tpks,tksc->tpc/dot_general | solution.py:117
  60.2 7.5 %all-to-all-start.8 = ((bf16[8,704,256]{2,1,0:T(8,128)(2,1)}), bf16[8,704,256]{2,1,0:T(8,128)(2,1)S(1)}, u32[]{:S(2)}, u32[]{:S(2)}) async-start(bf16[8,704,256]{2,1,0:T(8,128)(2,1)} %bitcast_convert_fusion.6), calls=%async_computation.8 | async-start | bytes 5767168 | tf_op jit(solution)/shard_map/cond/branch_0_fun/cond/branch_0_fun/cond/branch_1_fun/all_to_all | solution.py:113
  67.7 7.9 %convert_bitcast_fusion.9 = bf16[8,31,31,256]{3,1,0,2:T(8,128)(2,1)S(1)} fusion(bf16[31,240,2,256]{3,1,0,2:T(8,128)(2,1)} %bitcast.429, bf16[8,31,31,240]{3,2,1,0:T(8,128)(2,1)} %bitcast.411), kind=kOutput, calls=%fused_computation.147 | convolution fusion | flops 946669568 | bytes 11808768 | tf_op jit(solution)/shard_map/cond/branch_0_fun/cond/branch_0_fun/cond/branch_1_fun/tksj,sjc->tksc/dot_general | solution.py:340
  75.6 10.2 %bitcast_convert_fusion.7 = bf16[8,704,256]{2,1,0:T(8,128)(2,1)} fusion(bf16[8,31,31,256]{3,1,0,2:T(8,128)(2,1)S(1)} %convert_bitcast_fusion.9, s32[8,31,31]{2,1,0:T(8,128)S(1)} %eq.182), kind=kOutput, calls=%fused_computation.136 | convolution fusion | flops 2777978368 | bytes 6850592 | tf_op jit(solution)/shard_map/cond/branch_0_fun/cond/branch_0_fun/cond/branch_1_fun/tpks,tksc->tpc/dot_general | solution.py:117
  85.7 47.0 %all-to-all-done.8.refs_0_ = bf16[8,704,256]{2,1,0:T(8,128)(2,1)S(1)} async-done(((bf16[8,704,256]{2,1,0:T(8,128)(2,1)}), bf16[8,704,256]{2,1,0:T(8,128)(2,1)S(1)}, u32[]{:S(2)}, u32[]{:S(2)}) %all-to-all-start.8) | async-done | bytes 2883616 | tf_op jit(solution)/shard_map/cond/branch_0_fun/cond/branch_0_fun/cond/branch_1_fun/all_to_all | solution.py:113
  132.7 4.5 all-to-all-start.6
  137.6 3.8 convert_bitcast_fusion.6
  141.5 10.1 %bitcast_convert_fusion.5 = bf16[8,704,256]{2,1,0:T(8,128)(2,1)} fusion(bf16[8,31,31,256]{3,1,0,2:T(8,128)(2,1)S(1)} %convert_bitcast_fusion.6, s32[8,31,31]{2,1,0:T(8,128)S(1)} %eq.182), kind=kOutput, calls=%fused_computation.134 | convolution fusion | flops 2777978368 | bytes 6850592 | tf_op jit(solution)/shard_map/cond/branch_0_fun/cond/branch_0_fun/cond/branch_1_fun/tpks,tksc->tpc/dot_general | solution.py:117
  151.6 50.2 %all-to-all-done.6.refs_0_.refs_4_ = bf16[8,704,256]{2,1,0:T(8,128)(2,1)} async-done(((bf16[8,704,256]{2,1,0:T(8,128)(2,1)}), bf16[8,704,256]{2,1,0:T(8,128)(2,1)}, u32[]{:S(2)}, u32[]{:S(2)}) %all-to-all-start.6) | async-done | bytes 2883616 | tf_op jit(solution)/shard_map/cond/branch_0_fun/cond/branch_0_fun/cond/branch_1_fun/all_to_all | solution.py:113
  201.8 4.8 all-to-all-start.10
  206.6 3.9 convert_bitcast_fusion.5
  210.5 1.6 collective-permute-start.6
  212.1 10.1 %bitcast_convert_fusion.4 = bf16[8,704,256]{2,1,0:T(8,128)(2,1)} fusion(bf16[8,31,31,256]{3,1,0,2:T(8,128)(2,1)S(1)} %convert_bitcast_fusion.5, s32[8,31,31]{2,1,0:T(8,128)S(1)} %eq.182), kind=kOutput, calls=%fused_computation.133 | convolution fusion | flops 2777978368 | bytes 6850592 | tf_op jit(solution)/shard_map/cond/branch_0_fun/cond/branch_0_fun/cond/branch_1_fun/tpks,tksc->tpc/dot_general | solution.py:117
  222.2 49.0 %all-to-all-done.10.refs_8_ = bf16[8,704,256]{2,1,0:T(8,128)(2,1)} async-done(((bf16[8,704,256]{2,1,0:T(8,128)(2,1)}), bf16[8,704,256]{2,1,0:T(8,128)(2,1)}, u32[]{:S(2)}, u32[]{:S(2)}) %all-to-all-start.10) | async-done | bytes 2883616 | tf_op jit(solution)/shard_map/cond/branch_0_fun/cond/branch_0_fun/cond/branch_1_fun/all_to_all | solution.py:113
  271.2 4.5 all-to-all-start.11
  275.7 0.5 collective-permute-start.8
  276.4 0.7 convert_reduce_fusion.1
  277.1 1.6 collective-permute-start.9
  278.7 0.6 multiply_reduce_fusion.1
  279.6 0.8 reshape.1119.plan_ref
  280.4 0.6 broadcast_xor_fusion.1.owner_ref
  281.0 0.3 collective-permute-done.7.refs_2_.refs_6_
  281.3 4.1 collective-permute-done.8.refs_3_.refs_7_
  285.4 29.9 %coefficients.10 = bf16[8,704,256]{2,1,0:T(8,128)(2,1)} custom-call(s32[744]{0:T(1024)} %reshape.1119.plan_ref, s32[4]{0:T(128)} %broadcast_xor_fusion.1.owner_ref, bf16[8,704,256]{2,1,0:T(8,128)(2,1)} %all-to-all-done.6.refs_0_.refs_4_, bf16[8,704,256]{2,1,0:T(8,128)(2,1)} %collective-permute-done.6.refs_1_.refs_5_, ...), custom_call_target="tpu_custom_call" | custom-call | flops 6241124352 | bytes 30670848 | tf_op jit(solution)/shard_map/cond/branch_0_fun/cond/branch_0_fun/cond/branch_1_fun/coefficients/pallas_call | solution.py:247
  315.3 24.9 %all-to-all-done.11.refs_9_ = bf16[8,704,256]{2,1,0:T(8,128)(2,1)} async-done(((bf16[8,704,256]{2,1,0:T(8,128)(2,1)}), bf16[8,704,256]{2,1,0:T(8,128)(2,1)}, u32[]{:S(2)}, u32[]{:S(2)}) %all-to-all-start.11) | async-done | bytes 2883616 | tf_op jit(solution)/shard_map/cond/branch_0_fun/cond/branch_0_fun/cond/branch_1_fun/all_to_all | solution.py:113
  340.2 4.4 all-to-all-start.7
  344.7 0.5 collective-permute-start.11
  345.2 4.8 collective-permute-done.10.refs_2_
  350.0 1.6 copy-done.6
  351.6 2.7 collective-permute-done.11.refs_3_
  354.3 29.9 %coefficients.11 = bf16[8,704,256]{2,1,0:T(8,128)(2,1)} custom-call(s32[744]{0:T(1024)} %reshape.1119.plan_ref, s32[4]{0:T(128)} %broadcast_xor_fusion.1.owner_ref, bf16[8,704,256]{2,1,0:T(8,128)(2,1)} %copy-done.2, bf16[8,704,256]{2,1,0:T(8,128)(2,1)} %collective-permute-done.9.refs_1_, bf16[8,704,256]{2,1,0:T(8,128)(2,1)} %copy-done.6, ...), custom_call_target="tpu_custom_call" | custom-call | flops 6241124352 | bytes 30670848 | tf_op jit(solution)/shard_map/cond/branch_0_fun/cond/branch_0_fun/cond/branch_1_fun/coefficients/pallas_call | solution.py:247
  384.2 25.0 %all-to-all-done.7 = bf16[8,704,256]{2,1,0:T(8,128)(2,1)} async-done(((bf16[8,704,256]{2,1,0:T(8,128)(2,1)}), bf16[8,704,256]{2,1,0:T(8,128)(2,1)}, u32[]{:S(2)}, u32[]{:S(2)}) %all-to-all-start.7) | async-done | bytes 2883616 | tf_op jit(solution)/shard_map/cond/branch_0_fun/cond/branch_0_fun/cond/branch_1_fun/all_to_all | solution.py:113
  409.2 3.8 all-to-all-start.9
  413.2 4.5 copy.216
  417.6 3.2 pad.20
  420.8 6.4 %copy.229.table_ref = bf16[31,240,256]{2,1,0:T(8,128)(2,1)} copy(bf16[31,240,256]{1,2,0:T(8,128)(2,1)} %bitcast.423) | data formatting | bytes 7618560 | tf_op jit(solution)/shard_map/cond/branch_0_fun/cond/branch_0_fun/cond/branch_1_fun/reshape | solution.py:355
  427.2 5.6 %iota_compare_fusion.24 = pred[8,704,31,31]{1,3,2,0:T(8,128)(4,1)} fusion(s32[8,31,31]{2,1,0:T(8,128)S(1)} %eq.182), kind=kLoop, calls=%fused_computation.114 | loop fusion | flops 5412352 | bytes 5443104 | tf_op jit(solution)/shard_map/cond/branch_0_fun/cond/branch_0_fun/cond/branch_1_fun/eq | solution.py:313
  432.9 33.1 %mixing.5 = bf16[31,256,1024]{2,1,0:T(8,128)(2,1)} custom-call(s32[744]{0:T(1024)} %reshape.1119.plan_ref, s32[4]{0:T(128)} %broadcast_xor_fusion.1.owner_ref, bf16[8,704,256]{2,1,0:T(8,128)(2,1)} %copy-done.2, bf16[8,704,256]{2,1,0:T(8,128)(2,1)} %collective-permute-done.9.refs_1_, bf16[8,704,256]{2,1,0:T(8,128)(2,1)} %copy-done.6, ...), custom_call_target="tpu_custom_call" | custom-call | flops 12482248704 | bytes 45088768 | tf_op jit(solution)/shard_map/cond/branch_0_fun/cond/branch_0_fun/cond/branch_1_fun/mixing/pallas_call | solution.py:271
  466.0 7.8 %convert_bitcast_fusion.8.value_ref = bf16[31,8,32,256]{3,2,1,0:T(8,128)(2,1)} fusion(bf16[8,704,256]{2,1,0:T(8,128)(2,1)} %all-to-all-done.7, s32[8,32,31]{1,2,0:T(8,128)S(1)} %pad.21.clone), kind=kOutput, calls=%fused_computation.146 | convolution fusion | flops 2868133888 | bytes 6978560 | tf_op jit(solution)/shard_map/cond/branch_0_fun/cond/branch_0_fun/cond/branch_1_fun/tpks,tpc->stkc/dot_general | solution.py:368
  473.8 4.5 all-to-all-done.9
  478.3 11.3 %fusion.102.refs_0_ = bf16[31,240,256]{2,1,0:T(8,128)(2,1)} fusion(f32[240]{0:T(256)S(1)} %fusion.155, bf16[8,31,31,240]{3,2,1,0:T(8,128)(2,1)} %bitcast.413, pred[8,704,31,31]{1,3,2,0:T(8,128)(4,1)} %iota_compare_fusion.24, bf16[8,704,256]{2,1,0:T(8,128)(2,1)S(1)} %all-to-all-done.9), kind=kOutput, calls=%fused_computation.132 | convolution fusion | flops 3721603072 | bytes 15796416 | tf_op jit(solution)/shard_map/cond/branch_0_fun/cond/branch_0_fun/cond/branch_1_fun/tksj,tksc->sjc/dot_general | solution.py:375
  489.6 0.8 broadcast_in_dim.120.quad_ref
  490.4 13.7 %final.5 = bf16[31,240,2,256]{3,2,1,0:T(2,128)(2,1)} custom-call(bf16[31,240,256]{2,1,0:T(8,128)(2,1)} %copy.229.table_ref, bf16[31,8,32,256]{3,2,1,0:T(8,128)(2,1)} %convert_bitcast_fusion.8.value_ref, f32[240,256]{1,0:T(8,128)} %broadcast_in_dim.120.quad_ref, bf16[31,240,256]{2,1,0:T(8,128)(2,1)} %fusion.102.refs_0_), custom_call_target="tpu_custom_call" | custom-call | flops 975175680 | bytes 23109632 | tf_op jit(solution)/shard_map/cond/branch_0_fun/cond/branch_0_fun/cond/branch_1_fun/final/pallas_call | solution.py:138
  (62 shorter events, 2.6 us)
Async XLA Ops:
  6.0 7.4 %slice-start = ((s8[7618560]{0:T(1024)(128)(4,1)}), s8[4194304]{0:T(1024)(128)(4,1)S(1)}, s32[]{:S(2)}) async-start(s8[7618560]{0:T(1024)(128)(4,1)} %bitcast.404), calls=%async_computation.24 | async-start | bytes 8388608 | tf_op jit(solution)/shard_map/cond
  6.0 7.4 %slice-start.1 = ((s8[7618560]{0:T(1024)(128)(4,1)}), s8[3424256]{0:T(1024)(128)(4,1)S(1)}, s32[]{:S(2)}) async-start(s8[7618560]{0:T(1024)(128)(4,1)} %bitcast.404), calls=%async_computation.25 | async-start | bytes 6848512 | tf_op jit(solution)/shard_map/cond
  13.5 4.2 copy-start.14
  25.0 0.6 copy-start.17
  25.0 8.3 %copy-start.8 = (s32[31]{0:T(128)}, s32[31]{0:T(128)S(1)}, u32[]{:S(2)}) copy-start(s32[31]{0:T(128)S(1)} %get-tuple-element.102) | copy-start | bytes 376 | tf_op jit(solution)/shard_map/cond/branch_0_fun/cond/branch_0_fun/cond
  60.2 72.6 %all-to-all-start.8 = ((bf16[8,704,256]{2,1,0:T(8,128)(2,1)}), bf16[8,704,256]{2,1,0:T(8,128)(2,1)S(1)}, u32[]{:S(2)}, u32[]{:S(2)}) async-start(bf16[8,704,256]{2,1,0:T(8,128)(2,1)} %bitcast_convert_fusion.6), calls=%async_computation.8 | async-start | bytes 5767168 | tf_op jit(solution)/shard_map/cond/branch_0_fun/cond/branch_0_fun/cond/branch_1_fun/all_to_all | solution.py:113
  85.7 51.5 %copy-start.9 = (s32[31]{0:T(128)S(1)}, s32[31]{0:T(128)}, u32[]{:S(2)}) copy-start(s32[31]{0:T(128)} %copy-done.8) | copy-start | bytes 376 | tf_op jit(solution)/shard_map/cond/branch_0_fun/cond/branch_0_fun/cond
  132.7 211.9 %copy-start.2 = (bf16[8,704,256]{2,1,0:T(8,128)(2,1)}, bf16[8,704,256]{2,1,0:T(8,128)(2,1)S(1)}, u32[]{:S(2)}) copy-start(bf16[8,704,256]{2,1,0:T(8,128)(2,1)S(1)} %all-to-all-done.8.refs_0_) | copy-start | bytes 8650756 | tf_op jit(solution)/shard_map/cond/branch_0_fun/cond/branch_0_fun/cond
  132.7 69.0 %all-to-all-start.6 = ((bf16[8,704,256]{2,1,0:T(8,128)(2,1)}), bf16[8,704,256]{2,1,0:T(8,128)(2,1)}, u32[]{:S(2)}, u32[]{:S(2)}) async-start(bf16[8,704,256]{2,1,0:T(8,128)(2,1)} %bitcast_convert_fusion.7), calls=%async_computation.6 | async-start | bytes 5767168 | tf_op jit(solution)/shard_map/cond/branch_0_fun/cond/branch_0_fun/cond/branch_1_fun/all_to_all | solution.py:113
  201.8 69.4 %all-to-all-start.10 = ((bf16[8,704,256]{2,1,0:T(8,128)(2,1)}), bf16[8,704,256]{2,1,0:T(8,128)(2,1)}, u32[]{:S(2)}, u32[]{:S(2)}) async-start(bf16[8,704,256]{2,1,0:T(8,128)(2,1)} %bitcast_convert_fusion.5), calls=%async_computation.10 | async-start | bytes 5767168 | tf_op jit(solution)/shard_map/cond/branch_0_fun/cond/branch_0_fun/cond/branch_1_fun/all_to_all | solution.py:113
  210.5 65.2 %collective-permute-start.6 = (bf16[8,704,256]{2,1,0:T(8,128)(2,1)}, bf16[8,704,256]{2,1,0:T(8,128)(2,1)}, u32[]{:S(2)}, u32[]{:S(2)}) collective-permute-start(bf16[8,704,256]{2,1,0:T(8,128)(2,1)} %all-to-all-done.6.refs_0_.refs_4_), channel_id=1, source_target_pairs={{0,2},{1,3},{2,0},{3,1},{4,6},{5,7},{6,4},{7,5},{8,10},{9,11},{10,... | collective-permute-start | bytes 8650760 | tf_op jit(solution)/shard_map/cond/branch_0_fun/cond/branch_0_fun/cond/branch_1_fun/ppermute | solution.py:161
  222.1 54.1 %copy-start.23 = (s32[248]{0:T(256)S(1)}, s32[248]{0:T(256)}, u32[]{:S(2)}) copy-start(s32[248]{0:T(256)} %get-tuple-element.103) | copy-start | bytes 2980 | tf_op jit(solution)/shard_map/cond/branch_0_fun/cond/branch_0_fun/cond
  222.2 54.1 %copy-start.18 = (s32[248]{0:T(256)S(1)}, s32[248]{0:T(256)}, u32[]{:S(2)}) copy-start(s32[248]{0:T(256)} %copy-done.17) | copy-start | bytes 2980 | tf_op jit(solution)/shard_map/cond/branch_0_fun/cond/branch_0_fun/cond
  222.2 58.3 %copy-start.27 = (s32[4]{0:T(128)S(1)}, s32[4]{0:T(128)}, u32[]{:S(2)}) copy-start(s32[4]{0:T(128)} %get-tuple-element.104) | copy-start | bytes 52 | tf_op jit(solution)/shard_map/cond/branch_0_fun/cond/branch_0_fun/cond
  271.2 69.0 %all-to-all-start.11 = ((bf16[8,704,256]{2,1,0:T(8,128)(2,1)}), bf16[8,704,256]{2,1,0:T(8,128)(2,1)}, u32[]{:S(2)}, u32[]{:S(2)}) async-start(bf16[8,704,256]{2,1,0:T(8,128)(2,1)} %bitcast_convert_fusion.4), calls=%async_computation.11 | async-start | bytes 5767168 | tf_op jit(solution)/shard_map/cond/branch_0_fun/cond/branch_0_fun/cond/branch_1_fun/all_to_all | solution.py:113
  275.6 5.7 %collective-permute-start.7 = (bf16[8,704,256]{2,1,0:T(8,128)(2,1)}, bf16[8,704,256]{2,1,0:T(8,128)(2,1)}, u32[]{:S(2)}, u32[]{:S(2)}) collective-permute-start(bf16[8,704,256]{2,1,0:T(8,128)(2,1)} %all-to-all-done.6.refs_0_.refs_4_), channel_id=1, source_target_pairs={{0,1},{1,0},{2,3},{3,2},{4,5},{5,4},{6,7},{7,6},{8,9},{9,8},{10,11... | collective-permute-start | bytes 8650760 | tf_op jit(solution)/shard_map/cond/branch_0_fun/cond/branch_0_fun/cond/branch_1_fun/ppermute | solution.py:161
  275.7 9.7 %collective-permute-start.8 = (bf16[8,704,256]{2,1,0:T(8,128)(2,1)}, bf16[8,704,256]{2,1,0:T(8,128)(2,1)}, u32[]{:S(2)}, u32[]{:S(2)}) collective-permute-start(bf16[8,704,256]{2,1,0:T(8,128)(2,1)} %collective-permute-done.6.refs_1_.refs_5_), channel_id=1, source_target_pairs={{0,1},{1,0},{2,3},{3,2},{4,5},{5,4},{6,7},{7,6},{8,9},{9,8},{10,11... | collective-permute-start | bytes 8650760 | tf_op jit(solution)/shard_map/cond/branch_0_fun/cond/branch_0_fun/cond/branch_1_fun/ppermute | solution.py:161
  277.1 67.7 %collective-permute-start.9 = (bf16[8,704,256]{2,1,0:T(8,128)(2,1)S(1)}, bf16[8,704,256]{2,1,0:T(8,128)(2,1)}, u32[]{:S(2)}, u32[]{:S(2)}) collective-permute-start(bf16[8,704,256]{2,1,0:T(8,128)(2,1)S(1)} %all-to-all-done.8.refs_0_), channel_id=1, source_target_pairs={{0,2},{1,3},{2,0},{3,1},{4,6},{5,7},{6,4},{7,5},{8,10},{9,11},{10,... | collective-permute-start | bytes 8650760 | tf_op jit(solution)/shard_map/cond/branch_0_fun/cond/branch_0_fun/cond/branch_1_fun/ppermute | solution.py:161
  340.2 69.0 %all-to-all-start.7 = ((bf16[8,704,256]{2,1,0:T(8,128)(2,1)}), bf16[8,704,256]{2,1,0:T(8,128)(2,1)}, u32[]{:S(2)}, u32[]{:S(2)}) async-start(bf16[8,704,256]{2,1,0:T(8,128)(2,1)} %coefficients.10), calls=%async_computation.7 | async-start | bytes 5767168 | tf_op jit(solution)/shard_map/cond/branch_0_fun/cond/branch_0_fun/cond/branch_1_fun/all_to_all | solution.py:113
  344.7 5.3 collective-permute-start.10
  344.7 9.5 %collective-permute-start.11 = (bf16[8,704,256]{2,1,0:T(8,128)(2,1)}, bf16[8,704,256]{2,1,0:T(8,128)(2,1)}, u32[]{:S(2)}, u32[]{:S(2)}) collective-permute-start(bf16[8,704,256]{2,1,0:T(8,128)(2,1)} %collective-permute-done.9.refs_1_), channel_id=1, source_target_pairs={{0,1},{1,0},{2,3},{3,2},{4,5},{5,4},{6,7},{7,6},{8,9},{9,8},{10,11... | collective-permute-start | bytes 8650760 | tf_op jit(solution)/shard_map/cond/branch_0_fun/cond/branch_0_fun/cond/branch_1_fun/ppermute | solution.py:161
  350.0 1.6 copy-start.6
  409.2 69.1 %all-to-all-start.9 = ((bf16[8,704,256]{2,1,0:T(8,128)(2,1)}), bf16[8,704,256]{2,1,0:T(8,128)(2,1)S(1)}, u32[]{:S(2)}, u32[]{:S(2)}) async-start(bf16[8,704,256]{2,1,0:T(8,128)(2,1)} %coefficients.11), calls=%async_computation.9 | async-start | bytes 5767168 | tf_op jit(solution)/shard_map/cond/branch_0_fun/cond/branch_0_fun/cond/branch_1_fun/all_to_all | solution.py:113
